TPU v7x, 256 devices: a whole 4x4x8 slice. The times are simulated.
256 devices in a mesh: dp: 8 (over z), vocab: 32 (over y, x, core).
Axes of the slice: x: 4, y: 4, z: 8, core: 2. Of those that a mesh axis runs over, the one named last changes fastest.
Arguments:
- teacher_logits: bfloat16 [3072, 151552], P('dp', 'vocab'), may hold values from -40 to 320, as said below
- student_logits: bfloat16 [3072, 126976], P('dp', 'vocab'), may hold values from -40 to 320, as said below
- tile_dest: int32 [1184, 2], replicated, may hold values from 0 to 991, as said below
- tile_weight: bfloat16 [1184, 2, 128, 128], P('vocab'), may hold values from 0.0009994507 to 1
- token_mask: int32 [3072], P('dp'), may hold values from 0 to 1, as said below
Outputs:
- token_loss: float32 [3072], P('dp')
- mean_loss: float32 [], replicated
Inputs may be any that keep to these rules, and one draw needn't show every extreme that they name: `teacher_logits`: Real-valued logits. `student_logits`: Real-valued logits. `tile_dest`: row b names the student blocks of the 2 tiles of teacher block b. Student block s belongs to vocab index s // 31, teacher block b to vocab index b // 37. Of the tiles of the teacher blocks of one vocab index, at most 3 name student blocks of any one vocab index, and exactly 3 do for some vocab index. `token_mask`: at least one token has a 1.
All inputs are finite; a program needn't handle non-finite values.
Results may differ from a plain program's by a relative error of at most 0.0031.
Values may be sent and summed in bfloat16 or wider, within the bound.
No kernel may reach another device: no remote copies, remote signals or barrier semaphores. Data moves between devices by JAX's collectives and lax.ppermute only.
A program may use at most 128 MiB of HBM per device.

v0:
```python
import jax
import jax.numpy as jnp
from jax import lax
from jax.sharding import PartitionSpec as P

BLOCK = 128
VS = 126976
K = 2


SMOOTH = 0.1


def from_everyone(x, axis):
    length = lax.axis_size(axis)
    return lax.all_to_all(jnp.broadcast_to(x[None], (length, *x.shape)), axis, 0, 0, tiled=True)


def gathered_once(x, axis):
    leaves = jax.tree.leaves(x)
    sequence = sorted(range(len(leaves)), key=lambda k: -leaves[k].size)
    width = (1, *leaves[sequence[0]].shape)[-1]
    lines = [
        jnp.pad(leaves[k].reshape(-1), (0, -leaves[k].size % width)).reshape(-1, width)
        for k in sequence
    ]
    both, at, found = (from_everyone(jnp.concatenate(lines), axis), 0, {})
    for k, line in zip(sequence, lines):
        section = both[:, at : at + len(line)].reshape(len(both), -1)
        found[k] = section[:, : leaves[k].size].reshape(-1, *leaves[k].shape)
        at += len(line)
    numbers = iter(range(len(leaves)))
    return jax.tree.map(lambda _: found[next(numbers)], x)


def folded_in_pairs(pieces, combine):
    while len(jax.tree.leaves(pieces)[0]) > 1:
        pieces = jax.vmap(combine)(
            *(jax.tree.map(lambda part: part[side::2], pieces) for side in (0, 1))
        )
    return jax.tree.map(lambda part: part[0], pieces)


def merged(x, axis, combine):
    pieces = gathered_once(x, axis)
    return folded_in_pairs(pieces, combine)


def exchange_in_groups(x, axis, split_dim, concat_dim, work, item_dim, out_dim):
    items = jax.tree.leaves(x)[0].shape[item_dim]
    count = 2 if items % 2 == 0 else 1
    gathered = []
    for k in range(count):
        group = jax.tree.map(
            lambda a: lax.slice_in_dim(
                a, k * (items // count), (k + 1) * (items // count), axis=item_dim
            ),
            x,
        )
        gathered.append(
            work(
                lax.all_to_all(
                    group, axis, split_axis=split_dim, concat_axis=concat_dim, tiled=True
                )
            )
        )
    return jax.tree.map(lambda *parts: jnp.concatenate(parts, axis=out_dim), *gathered)


def taken_together(x, axis):
    everything = from_everyone(x, axis)
    return jnp.sum(everything, axis=0)


def pair_join(former, latter):
    maximum = jnp.maximum(former[0], latter[0])
    return (
        maximum,
        former[1] * jnp.exp(former[0] - maximum) + latter[1] * jnp.exp(latter[0] - maximum),
    )


def folded_join(former, latter):
    maximum, totals = pair_join((former[0], former[1]), (latter[0], latter[1]))
    return (maximum, totals, former[2] + latter[2], former[3] + latter[3])


def teacher_norm(values):
    local_top = jnp.max(values, axis=1)
    local_sum = jnp.sum(jnp.exp(values - local_top[:, None]), axis=1)
    return merged((local_top, local_sum), "vocab", pair_join)


def routing(tile_dest, group_size, sb_dev):
    flat_dest = tile_dest.reshape(group_size, -1)
    owners = flat_dest // sb_dev
    local_block = flat_dest % sb_dev
    owner_hits = (owners[:, :, None] == jnp.arange(group_size, dtype=jnp.int32)).astype(jnp.int32)
    earlier = jnp.cumsum(owner_hits, axis=1) - owner_hits
    slot_rank = jnp.sum(owner_hits * earlier, axis=2)
    return (owners, local_block, slot_rank)


def local(teacher_logits, student_logits, tile_dest, tile_weight, token_mask):
    group_size = lax.axis_size("vocab")
    my_index = lax.axis_index("vocab")
    tok_rows = teacher_logits.shape[0]
    tb_dev = teacher_logits.shape[1] // BLOCK
    sb_dev = student_logits.shape[1] // BLOCK
    tile_count = tb_dev * K
    capacity = (tile_count + group_size - 1) // group_size
    teacher_vals = teacher_logits.astype(jnp.float32)
    teacher_max, teacher_sum = teacher_norm(teacher_vals)
    teacher_prob = (jnp.exp(teacher_vals - teacher_max[:, None]) / teacher_sum[:, None]).astype(
        jnp.bfloat16
    )
    prob_blocks = teacher_prob.reshape(tok_rows, tb_dev, BLOCK)
    weights = tile_weight.astype(jnp.float32)
    mapping = (weights / jnp.sum(weights, axis=(1, 3), keepdims=True)).astype(jnp.bfloat16)
    owners, local_block, slot_rank = routing(tile_dest, group_size, sb_dev)
    my_owner = lax.dynamic_index_in_dim(owners, my_index, 0, keepdims=False)
    my_rank = lax.dynamic_index_in_dim(slot_rank, my_index, 0, keepdims=False)
    my_slot = my_owner * capacity + my_rank
    placement = (
        jnp.arange(group_size * capacity, dtype=jnp.int32)[:, None] == my_slot[None, :]
    ).astype(jnp.bfloat16)
    mine = owners == my_index
    slot_hit = (
        (slot_rank[:, :, None] == jnp.arange(capacity, dtype=jnp.int32)) & mine[:, :, None]
    ).astype(jnp.float32)
    block_hit = (local_block[:, :, None] == jnp.arange(sb_dev, dtype=jnp.int32)).astype(jnp.float32)
    slot_table = (
        jnp.einsum("ric,rij->rcj", slot_hit, block_hit)
        .reshape(group_size * capacity, sb_dev)
        .astype(jnp.bfloat16)
    )

    def collect(received):
        item_count = received.shape[2]
        flat_items = received.reshape(group_size * capacity, item_count, BLOCK)
        summed = jnp.einsum(
            "snd,sj->njd", flat_items, slot_table, preferred_element_type=jnp.float32
        )
        return summed.reshape(item_count, sb_dev * BLOCK)

    partial_value = jnp.einsum(
        "tbc,bkcd->bktd", prob_blocks, mapping, preferred_element_type=jnp.float32
    )
    partial_value = partial_value.astype(jnp.bfloat16).reshape(tile_count, tok_rows, BLOCK)
    outgoing = jnp.einsum(
        "si,itd->std", placement, partial_value, preferred_element_type=jnp.float32
    )
    outgoing = outgoing.astype(jnp.bfloat16).reshape(group_size, capacity, tok_rows, BLOCK)
    mapped = exchange_in_groups(outgoing, "vocab", 0, 0, collect, 2, 0)
    target = (1.0 - SMOOTH) * mapped + SMOOTH / VS
    student_vals = student_logits.astype(jnp.float32)
    local_top = jnp.max(student_vals, axis=1)
    local_sum = jnp.sum(jnp.exp(student_vals - local_top[:, None]), axis=1)
    cross_part = jnp.sum(target * (jnp.log(target) - student_vals), axis=1)
    target_mass = jnp.sum(target, axis=1)
    student_max, student_sum, cross_sum, mass_sum = merged(
        (local_top, local_sum, cross_part, target_mass), "vocab", folded_join
    )
    token_kl = cross_sum + (student_max + jnp.log(student_sum)) * mass_sum
    mask_vals = token_mask.astype(jnp.float32)
    token_loss = mask_vals * token_kl
    loss_total, mask_total = (
        taken_together(jnp.sum(token_loss), "dp"),
        taken_together(jnp.sum(mask_vals), "dp"),
    )
    return (token_loss, loss_total / mask_total)


def solution(mesh):
    in_specs = (P("dp", "vocab"), P("dp", "vocab"), P(), P("vocab", None, None, None), P("dp"))
    out_specs = (P("dp"), P())
    return jax.shard_map(local, mesh=mesh, in_specs=in_specs, out_specs=out_specs, check_vma=False)
```

profile of v0, /device:TPU:1, one launch (start us, length us, event | category | flops | bytes accessed | tf_op | source)
XLA Modules:
  0.0 258.6 jit_solution(9440288344838982405)
XLA Ops:
  0.6 2.6 %reduce_max.40 = bf16[384]{0:T(512)(128)(2,1)S(1)} reduce(bf16[384,4736]{1,0:T(8,128)(2,1)} %param.5, bf16[]{:T(256)} %constant.37.clone.1), dimensions={1}, to_apply=%region_5.6 | reduce | flops 1818240 | bytes 3638018 | tf_op jit(solution)/shard_map/reduce_max | solution.py:89
  3.3 6.0 %copy.179 = bf16[384,4736]{0,1:T(8,128)(2,1)} copy(bf16[384,4736]{1,0:T(8,128)(2,1)} %param.5) | data formatting | bytes 7274496 | tf_op args[0]
  9.3 3.3 %fusion.1 = f32[384]{0:T(512)S(1)} fusion(bf16[384,4736]{0,1:T(8,128)(2,1)} %copy.179, f32[384]{0:T(512)S(1)} %reduce_max.45), kind=kLoop, calls=%fused_computation.5 | loop fusion | flops 5455488 | bytes 3640320 | tf_op jit(solution)/shard_map/reduce_sum | solution.py:90
  13.2 8.6 %all-to-all-start = ((f32[32,2,384]{2,1,0:T(2,128)}), f32[32,2,384]{2,1,0:T(2,128)S(1)}, u32[]{:S(2)}, u32[]{:S(2)}) async-start(f32[32,2,384]{2,1,0:T(2,128)} %broadcast_in_dim.8), calls=%async_computation | async-start | bytes 196608 | tf_op jit(solution)/shard_map/all_to_all | solution.py:16
  24.3 2.0 select_reduce_fusion
  26.4 2.9 %all-to-all-done = f32[32,2,384]{2,1,0:T(2,128)S(1)} async-done(((f32[32,2,384]{2,1,0:T(2,128)}), f32[32,2,384]{2,1,0:T(2,128)S(1)}, u32[]{:S(2)}, u32[]{:S(2)}) %all-to-all-start) | async-done | bytes 98336 | tf_op jit(solution)/shard_map/all_to_all | solution.py:16
  29.8 3.4 %fusion.4 = bf16[384,4736]{0,1:T(8,128)(2,1)S(1)} fusion(bf16[384,4736]{0,1:T(8,128)(2,1)} %copy.179, f32[384]{0:T(512)S(1)} %get-tuple-element.6, f32[384]{0:T(512)S(1)} %get-tuple-element.5), kind=kLoop, calls=%fused_computation.8 | loop fusion | flops 7274496 | bytes 7277568 | tf_op jit(solution)/shard_map/convert_element_type | solution.py:114
  33.2 5.2 %convolution_convert_fusion.1 = bf16[37,2,128,384]{3,2,1,0:T(8,128)(2,1)} fusion(bf16[384,37,128,1]{0,2,3,1:T(8,128)(2,1)S(1)} %bitcast.59, bf16[37,2,128,128]{3,2,1,0:T(8,128)(2,1)S(1)} %copy-done.2, f32[37,128]{1,0:T(8,128)S(1)} %convert_reduce_fusion), kind=kOutput, calls=%fused_computation.10 | convolution fusion | flops 938409984 | bytes 13355520 | tf_op jit(solution)/shard_map/tbc,bkcd->bktd/dot_general | solution.py:146
  38.4 10.7 %copy.183 = bf16[74,384,128]{2,0,1:T(8,128)(2,1)} copy(bf16[74,384,128]{1,2,0:T(8,128)(2,1)} %bitcast.58) | data formatting | bytes 14548992 | tf_op jit(solution)/shard_map/reshape | solution.py:149
  49.1 9.6 %convolution_convert_fusion = bf16[96,384,128]{2,0,1:T(8,128)(2,1)} fusion(bf16[74,384,128]{2,0,1:T(8,128)(2,1)} %copy.183, s32[74]{0:T(128)S(1)} %add_bitcast_fusion), kind=kOutput, calls=%fused_computation.9 | convolution fusion | flops 703077312 | bytes 16711976 | tf_op jit(solution)/shard_map/si,itd->std/dot_general | solution.py:150
  58.7 11.0 %copy.184 = bf16[96,384,128]{2,1,0:T(8,128)(2,1)} copy(bf16[96,384,128]{2,0,1:T(8,128)(2,1)} %convolution_convert_fusion) | data formatting | bytes 18874368 | tf_op jit(solution)/shard_map/convert_element_type | solution.py:153
  69.7 7.9 %fusion.43 = (bf16[32,3,192,128]{3,2,1,0:T(8,128)(2,1)S(1)}, bf16[32,3,192,128]{3,2,1,0:T(8,128)(2,1)}) fusion(bf16[32,3,384,128]{3,2,1,0:T(8,128)(2,1)} %bitcast.53), kind=kLoop, calls=%fused_computation.88 | loop fusion | bytes 18874368 | tf_op jit(solution)/shard_map/slice | solution.py:55
  77.6 60.9 %all_to_all.32 = bf16[32,3,192,128]{3,2,1,0:T(8,128)(2,1)} all-to-all(bf16[32,3,192,128]{3,2,1,0:T(8,128)(2,1)S(1)} %get-tuple-element.27), channel_id=1, replica_groups=mesh['dp'=8,'vocab'=32] {'vocab'}, dimensions={0} | all-to-all | bytes 9437184 | tf_op jit(solution)/shard_map/all_to_all | solution.py:62
  138.5 5.2 %all-to-all-start.2 = ((bf16[32,3,192,128]{3,2,1,0:T(8,128)(2,1)}), bf16[32,3,192,128]{3,2,1,0:T(8,128)(2,1)}, u32[]{:S(2)}, u32[]{:S(2)}) async-start(bf16[32,3,192,128]{3,2,1,0:T(8,128)(2,1)} %get-tuple-element.28), calls=%async_computation.2 | async-start | bytes 9437184 | tf_op jit(solution)/shard_map/all_to_all | solution.py:62
  144.5 5.4 %fusion.13 = f32[31,192,128,1]{2,0,3,1:T(8,128)S(1)} fusion(bf16[32,3,192,128]{3,2,1,0:T(8,128)(2,1)} %all_to_all.32, bf16[32,3,31]{2,1,0:T(4,128)(2,1)S(1)} %fusion.23), kind=kOutput, calls=%fused_computation.22 | convolution fusion | flops 146276352 | bytes 7771968 | tf_op jit(solution)/shard_map/snd,sj->njd/dot_general | solution.py:141
  150.0 4.2 %copy.232 = f32[24,8,31,128]{3,1,2,0:T(8,128)} copy(f32[24,8,31,128]{3,2,1,0:T(8,128)S(1)} %bitcast.55) | data formatting | bytes 6094848
  154.2 45.3 %all-to-all-done.2 = bf16[32,3,192,128]{3,2,1,0:T(8,128)(2,1)} async-done(((bf16[32,3,192,128]{3,2,1,0:T(8,128)(2,1)}), bf16[32,3,192,128]{3,2,1,0:T(8,128)(2,1)}, u32[]{:S(2)}, u32[]{:S(2)}) %all-to-all-start.2) | async-done | bytes 4718624 | tf_op jit(solution)/shard_map/all_to_all | solution.py:62
  199.5 5.4 %fusion.11 = f32[31,192,128,1]{2,0,3,1:T(8,128)S(1)} fusion(bf16[32,3,192,128]{3,2,1,0:T(8,128)(2,1)} %all-to-all-done.2, bf16[32,3,31]{2,1,0:T(4,128)(2,1)S(1)} %fusion.23), kind=kOutput, calls=%fused_computation.20 | convolution fusion | flops 146276352 | bytes 7771968 | tf_op jit(solution)/shard_map/snd,sj->njd/dot_general | solution.py:141
  205.0 2.7 %copy.231 = f32[24,8,31,128]{3,1,2,0:T(8,128)S(1)} copy(f32[24,8,31,128]{3,2,1,0:T(8,128)S(1)} %bitcast.54) | data formatting | bytes 6094848
  207.7 4.0 %fusion.8 = (f32[384]{0:T(512)S(1)}, f32[384]{0:T(512)S(1)}, f32[384]{0:T(512)S(1)}) fusion(bf16[384,3968]{1,0:T(8,128)(2,1)S(1)} %copy-done, f32[192,3968]{1,0:T(8,128)S(1)} %bitcast.57, f32[192,3968]{1,0:T(8,128)S(1)} %bitcast.56, f32[384]{0:T(512)S(1)} %reduce_max.44), kind=kLoop, calls=%fused_computation.14 | loop fusion | flops 15235968 | bytes 9148416 | tf_op jit(solution)/shard_map/reduce_sum | solution.py:159
  211.7 15.4 %all_to_all.33 = f32[32,4,384]{2,1,0:T(4,128)S(1)} all-to-all(f32[32,4,384]{2,1,0:T(4,128)S(1)} %broadcast_in_dim.9), channel_id=1, replica_groups=mesh['dp'=8,'vocab'=32] {'vocab'}, dimensions={0} | all-to-all | bytes 393216 | tf_op jit(solution)/shard_map/all_to_all | solution.py:16
  230.1 14.5 %all_to_all.34 = f32[8,1,1]{2,1,0:T(1,128)S(1)} all-to-all(f32[8,1,1]{2,1,0:T(1,128)S(1)} %broadcast_in_dim.11), channel_id=1, replica_groups=mesh['dp'=8,'vocab'=32] {'dp'}, dimensions={0} | all-to-all | bytes 64 | tf_op jit(solution)/shard_map/all_to_all | solution.py:16
  245.8 3.3 %all-to-all-start.4 = ((f32[8,1,1]{2,1,0:T(1,128)}), f32[8,1,1]{2,1,0:T(1,128)S(1)}, u32[]{:S(2)}, u32[]{:S(2)}) async-start(f32[8,1,1]{2,1,0:T(1,128)} %broadcast_in_dim.10), calls=%async_computation.4 | async-start | bytes 8192 | tf_op jit(solution)/shard_map/all_to_all | solution.py:16
  249.8 5.8 %all-to-all-done.4 = f32[8,1,1]{2,1,0:T(1,128)S(1)} async-done(((f32[8,1,1]{2,1,0:T(1,128)}), f32[8,1,1]{2,1,0:T(1,128)S(1)}, u32[]{:S(2)}, u32[]{:S(2)}) %all-to-all-start.4) | async-done | bytes 64 | tf_op jit(solution)/shard_map/all_to_all | solution.py:16
  (116 shorter events, 9.8 us)
Async XLA Ops:
  3.2 18.6 %copy-start.3 = (s32[1184,2]{0,1:T(2,128)S(1)}, s32[1184,2]{0,1:T(2,128)}, u32[]{:S(2)}) copy-start(s32[1184,2]{0,1:T(2,128)} %param.7) | copy-start | bytes 28420
  3.3 18.7 %copy-start.2 = (bf16[37,2,128,128]{3,2,1,0:T(8,128)(2,1)S(1)}, bf16[37,2,128,128]{3,2,1,0:T(8,128)(2,1)}, u32[]{:S(2)}) copy-start(bf16[37,2,128,128]{3,2,1,0:T(8,128)(2,1)} %param.8) | copy-start | bytes 7274500
  13.2 16.0 %all-to-all-start = ((f32[32,2,384]{2,1,0:T(2,128)}), f32[32,2,384]{2,1,0:T(2,128)S(1)}, u32[]{:S(2)}, u32[]{:S(2)}) async-start(f32[32,2,384]{2,1,0:T(2,128)} %broadcast_in_dim.8), calls=%async_computation | async-start | bytes 196608 | tf_op jit(solution)/shard_map/all_to_all | solution.py:16
  138.5 5.2 %copy-start = (bf16[384,3968]{1,0:T(8,128)(2,1)S(1)}, bf16[384,3968]{1,0:T(8,128)(2,1)}, u32[]{:S(2)}) copy-start(bf16[384,3968]{1,0:T(8,128)(2,1)} %param.6) | copy-start | bytes 9142276
  138.5 61.0 %all-to-all-start.2 = ((bf16[32,3,192,128]{3,2,1,0:T(8,128)(2,1)}), bf16[32,3,192,128]{3,2,1,0:T(8,128)(2,1)}, u32[]{:S(2)}, u32[]{:S(2)}) async-start(bf16[32,3,192,128]{3,2,1,0:T(8,128)(2,1)} %get-tuple-element.28), calls=%async_computation.2 | async-start | bytes 9437184 | tf_op jit(solution)/shard_map/all_to_all | solution.py:62
  204.9 2.7 %copy-start.1 = (f32[24,8,31,128]{3,1,2,0:T(8,128)S(1)}, f32[24,8,31,128]{3,1,2,0:T(8,128)}, u32[]{:S(2)}) copy-start(f32[24,8,31,128]{3,1,2,0:T(8,128)} %copy.232) | copy-start | bytes 9142276
  207.6 20.5 %copy-start.4 = (s32[384]{0:T(512)S(1)}, s32[384]{0:T(512)}, u32[]{:S(2)}) copy-start(s32[384]{0:T(512)} %param.9) | copy-start | bytes 4612
  245.8 9.8 %all-to-all-start.4 = ((f32[8,1,1]{2,1,0:T(1,128)}), f32[8,1,1]{2,1,0:T(1,128)S(1)}, u32[]{:S(2)}, u32[]{:S(2)}) async-start(f32[8,1,1]{2,1,0:T(1,128)} %broadcast_in_dim.10), calls=%async_computation.4 | async-start | bytes 8192 | tf_op jit(solution)/shard_map/all_to_all | solution.py:16
where the time goes:
time: 260 us; the launch traced here: 259 us
  blocking collectives  90.8 us (35%)
  waiting for transfers between devices  54 us (21%)
  local copies, waits for them, and re-layouts  48.1 us (18%)
  matrix products  25.9 us (10%)
  other arithmetic  19.3 us (7%)
  starting transfers between devices  17.1 us (7%)
  between operations  3.41 us (1%)
    all_to_all x1, blocking collectives, exchange_in_groups(): lax.all_to_all(group, axis, split_axis=split_dim, concat_axis=concat_dim,...  60.9 us
    all_to_all x1, waiting for transfers between devices, exchange_in_groups(): lax.all_to_all(group, axis, split_axis=split_dim, concat_axis=concat_dim,...  45.3 us
    all_to_all x2, blocking collectives, from_everyone(): lax.all_to_all(jnp.broadcast_to(x[None], (length, *x.shape)), axis, 0, 0,...  29.9 us
    unnamed x17, local copies, waits for them, and re-layouts  13 us
    all_to_all x2, starting transfers between devices, from_everyone(): lax.all_to_all(jnp.broadcast_to(x[None], (length, *x.shape)), axis, 0, 0,...  11.9 us
    convert_element_type x1, local copies, waits for them, and re-layouts, local(): outgoing.astype(jnp.bfloat16).reshape(group_size, capacity, tok_rows, BLOCK)  11 us
    dot_general x2, matrix products, collect(): jnp.einsum('snd,sj->njd', flat_items, slot_table, preferred_element_type=...  10.9 us
    reshape x1, local copies, waits for them, and re-layouts, local(): partial_value.astype(jnp.bfloat16).reshape(tile_count, tok_rows, BLOCK)  10.7 us
  transfers between devices with their start and end apart: 3, of which 3 were waited for; matrix products, arithmetic and copies ran while one was open for 6% of the time, Pallas kernels for 0%

commit v1 on v0

v1 whole, which is shorter than its diff:
```python
import functools

import jax
import jax.numpy as jnp
from jax import lax
from jax.experimental import pallas as pl
from jax.experimental.pallas import tpu as pltpu
from jax.sharding import PartitionSpec as P

BLOCK = 128
VS = 126976
K = 2
CAP = 3
SMOOTH = 0.1
LANES = 128
STAT_ROWS = 16
F32 = jnp.float32
BF16 = jnp.bfloat16


def iota(shape, dim):
    return lax.broadcasted_iota(jnp.int32, shape, dim)


def selector(mask_row, rows, first):
    tokens = mask_row.shape[1]
    before = (iota((tokens, tokens), 0) < iota((tokens, tokens), 1)).astype(F32).astype(BF16)
    kept = jnp.broadcast_to(mask_row.astype(F32), (16, tokens)).astype(BF16)
    rank = jnp.dot(kept, before, preferred_element_type=F32)[0:1]
    wanted = (iota((rows, tokens), 0) + first).astype(F32)
    hit = (wanted == jnp.broadcast_to(rank, (rows, tokens))) & (
        jnp.broadcast_to(mask_row, (rows, tokens)) > 0
    )
    return hit.astype(F32).astype(BF16)


def thirds(value):
    high = value.astype(BF16).astype(F32)
    middle = (value - high).astype(BF16).astype(F32)
    low = (value - high - middle).astype(BF16).astype(F32)
    return high, middle, low


def in_lanes(columns, rows):
    lane = iota((rows, LANES), 1)
    out = jnp.zeros((rows, LANES), F32)
    for v, column in enumerate(columns):
        if column is not None:
            out = jnp.where(lane == v, jnp.broadcast_to(column, (rows, LANES)), out)
    return out


def pieces_of(total, parts):
    cuts = [total * i // parts for i in range(parts + 1)]
    return list(zip(cuts[:-1], cuts[1:]))


def picked(sel_ref, src_ref, dst_ref, top_ref, blocks, waits):
    top_ref[...] = jnp.full(top_ref.shape, -jnp.inf, F32)

    def one(start, width):
        got = jnp.dot(sel_ref[...], src_ref[:, pl.ds(start, width)], preferred_element_type=F32)
        dst_ref[:, pl.ds(start, width)] = got.astype(BF16)
        top = top_ref[...]
        for i in range(width // BLOCK):
            top = jnp.maximum(top, got[:, i * BLOCK : (i + 1) * BLOCK])
        top_ref[...] = top

    for (lo, hi), wait in waits:
        wait()

        def body(i, carry):
            one(pl.multiple_of(i * 2 * BLOCK, 2 * BLOCK), 2 * BLOCK)
            return carry

        lax.fori_loop(lo, hi, body, 0)
    if blocks % 2:
        one((blocks - 1) * BLOCK, BLOCK)


def column_waits(hbm, buf, sems, blocks, parts):
    out = []
    runs = pieces_of(blocks // 2, parts)
    for c, (lo, hi) in enumerate(runs):
        end = hi * 2 * BLOCK if c < len(runs) - 1 else blocks * BLOCK
        where = (slice(None), pl.ds(lo * 2 * BLOCK, end - lo * 2 * BLOCK))
        copy = pltpu.make_async_copy(hbm.at[where], buf.at[where], sems.at[c])
        copy.start()
        out.append(((lo, hi), copy.wait))
    return out


def send_kernel(
    rows, first, sb_dev,
    me_ref, dest_ref, mask_ref, x_hbm, w_hbm, send_hbm,
    x_buf, w_buf, sel, xc, maps, stage, stat_cols, stat, top, total, used,
    w_sem, x_sem, out_sem, stat_sem,
):
    blocks = w_buf.shape[0]
    peers = send_hbm.shape[0]
    w_copy = pltpu.make_async_copy(w_hbm, w_buf, w_sem)
    w_copy.start()
    waits = column_waits(x_hbm, x_buf, x_sem, blocks, 4)
    sel[...] = selector(mask_ref[...], rows, first)

    def clear(i, carry):
        used[i] = 0
        return carry

    lax.fori_loop(0, peers, clear, 0)
    w_copy.wait()

    def weights(b, carry):
        both = jnp.concatenate([w_buf[b, k].astype(F32) for k in range(K)], axis=1)
        scale = 1.0 / jnp.sum(both, axis=1, keepdims=True)
        maps[b] = (both * scale).astype(BF16)
        return carry

    lax.fori_loop(0, blocks, weights, 0)
    picked(sel, x_buf, xc, top, blocks, waits)
    highest = jnp.max(top[...], axis=1, keepdims=True)
    top[...] = jnp.broadcast_to(highest, top.shape)
    total[...] = jnp.zeros(total.shape, F32)
    base = me_ref[0] * blocks

    def block(b, carry):
        raised = jnp.exp(xc[:, pl.ds(pl.multiple_of(b * BLOCK, BLOCK), BLOCK)].astype(F32) - top[...])
        total[...] += raised
        mapped = jnp.dot(raised.astype(BF16), maps[b], preferred_element_type=F32)
        for k in range(K):
            stage[K * b + k] = mapped[:, k * BLOCK : (k + 1) * BLOCK].astype(BF16)
            owner = lax.div(dest_ref[k, base + b], sb_dev)
            rank = used[owner]
            used[owner] = rank + 1
            pltpu.make_async_copy(
                stage.at[K * b + k],
                send_hbm.at[owner, pl.ds(pl.multiple_of(rank * rows, 16), rows)],
                out_sem.at[K * b + k],
            ).start()
        return carry

    lax.fori_loop(0, blocks, block, 0)
    summed = jnp.sum(total[...], axis=1, keepdims=True)
    stat_cols[...] = jnp.zeros(stat_cols.shape, F32)
    stat_cols[0:rows] = in_lanes((highest, *thirds(summed)), rows)
    for q in range(stat_cols.shape[0] // LANES):
        turned = stat_cols[q * LANES : (q + 1) * LANES].T
        stat[q * STAT_ROWS : (q + 1) * STAT_ROWS] = turned[:STAT_ROWS].astype(BF16)

    def stat_copy(d):
        return pltpu.make_async_copy(
            stat, send_hbm.at[d, pl.ds(CAP * rows, stat.shape[0])], stat_sem.at[d]
        )

    def stat_start(d, carry):
        stat_copy(d).start()
        return carry

    def stat_wait(d, carry):
        stat_copy(d).wait()
        return carry

    def tile_wait(i, carry):
        pltpu.make_async_copy(
            stage.at[i], send_hbm.at[0, pl.ds(0, rows)], out_sem.at[i]
        ).wait()
        return carry

    lax.fori_loop(0, peers, stat_start, 0)
    lax.fori_loop(0, K * blocks, tile_wait, 0)
    lax.fori_loop(0, peers, stat_wait, 0)


def student_kernel(
    rows, first, peers, tb_dev,
    me_ref, dest_ref, mask_ref, s_hbm,
    picked_ref, stat_ref, count_ref, slot_ref,
    s_buf, sel, cols, top, s_sem,
):
    blocks = s_buf.shape[1] // BLOCK
    waits = column_waits(s_hbm, s_buf, s_sem, blocks, 2)
    sel[...] = selector(mask_ref[...], rows, first)
    picked(sel, s_buf, picked_ref, top, blocks, waits)
    highest = jnp.max(top[...], axis=1, keepdims=True)

    def block(b, carry):
        at = pl.ds(pl.multiple_of(b * BLOCK, BLOCK), BLOCK)
        return carry + jnp.exp(picked_ref[:, at].astype(F32) - highest)

    total = lax.fori_loop(0, blocks, block, jnp.zeros((rows, BLOCK), F32))
    cols[...] = jnp.zeros(cols.shape, F32)
    cols[0:rows] = in_lanes((None, None, highest, jnp.sum(total, axis=1, keepdims=True)), rows)
    for q in range(cols.shape[0] // LANES):
        at = slice(q * LANES, (q + 1) * LANES)
        stat_ref[:, at] = cols[at].T[:8]

    def clear(i, carry):
        count_ref[i] = 0
        return carry

    lax.fori_loop(0, count_ref.shape[0], clear, 0)
    low = me_ref[0] * blocks

    def source(r, carry):
        def tile(b, rank):
            for k in range(K):
                near = dest_ref[k, r * tb_dev + b] - low
                mine = (near >= 0) & (near < blocks)

                @pl.when(mine)
                def _():
                    seen = count_ref[near]
                    slot_ref[near * (peers * CAP) + seen] = r * 4 + rank
                    count_ref[near] = seen + 1

                rank = rank + mine.astype(jnp.int32)
            return rank

        lax.fori_loop(0, tb_dev, tile, jnp.int32(0))
        return carry

    lax.fori_loop(0, peers, source, 0)


def combine_kernel(
    rows, chunk,
    count_ref, slot_ref, recv_hbm, s_ref, s_stat_ref, out_ref,
    buf, stat, stat32, share, spread, cols, sems, stat_sem,
):
    peers = recv_hbm.shape[0]
    blocks = s_ref.shape[1] // BLOCK
    stat_copy = pltpu.make_async_copy(
        recv_hbm.at[:, pl.ds(CAP * rows, stat.shape[1])], stat, stat_sem
    )
    stat_copy.start()
    copies = []
    for q in range(rows // chunk):
        for r in range(CAP):
            copy = pltpu.make_async_copy(
                recv_hbm.at[:, pl.ds(r * rows + q * chunk, chunk)],
                buf.at[r, :, pl.ds(q * chunk, chunk)],
                sems.at[q, r],
            )
            copy.start()
            copies.append(copy)
    stat_copy.wait()
    per = stat.shape[1]
    stat32[...] = stat[...].astype(F32).reshape(stat32.shape)
    for q in range(per // STAT_ROWS):
        highest, high, middle, low = (
            stat32[pl.ds(q * STAT_ROWS + v, peers, stride=per), :] for v in range(4)
        )
        raised = jnp.exp(highest - jnp.max(highest, axis=0, keepdims=True))
        total = jnp.sum(raised * ((high + middle) + low), axis=0, keepdims=True)
        part = raised * ((1.0 - SMOOTH) / total)
        padded = jnp.concatenate([part, jnp.zeros((LANES - peers, LANES), F32)], axis=0)
        share[q * LANES : (q + 1) * LANES] = padded.T
    cols[...] = jnp.zeros(cols.shape, F32)
    for q in range(rows // chunk):
        at = slice(q * chunk, (q + 1) * chunk)
        mine = share[at]
        for r in range(peers):
            spread[r] = jnp.broadcast_to(mine[:, r : r + 1], (chunk, LANES))
        for r in range(CAP):
            copies[q * CAP + r].wait()

        def block(j, carry):
            cross, mass = carry

            def add(n, acc):
                entry = slot_ref[j * (peers * CAP) + n]
                source = lax.shift_right_logical(entry, 2)
                piece = buf[entry & 3, source, at]
                return acc + spread[source] * piece.astype(F32)

            mapped = lax.fori_loop(0, count_ref[j], add, jnp.zeros((chunk, LANES), F32))
            target = mapped + SMOOTH / VS
            student = s_ref[at, pl.ds(pl.multiple_of(j * BLOCK, BLOCK), BLOCK)].astype(F32)
            return cross + target * (jnp.log(target) - student), mass + target

        zero = jnp.zeros((chunk, LANES), F32)
        cross, mass = lax.fori_loop(0, blocks, block, (zero, zero))
        cols[at] = in_lanes(
            (jnp.sum(cross, axis=1, keepdims=True), jnp.sum(mass, axis=1, keepdims=True)), chunk
        )
    for q in range(cols.shape[0] // LANES):
        at = slice(q * LANES, (q + 1) * LANES)
        values = cols[at].T[:8] + s_stat_ref[:, at]
        per = 8 * (cols.shape[0] // LANES)
        for d in range(peers):
            out_ref[d * per + q * 8 : d * per + (q + 1) * 8] = values


def loss_kernel(rows, first, all_ref, mask_ref, loss_ref, sums_ref):
    tokens = mask_ref.shape[1]
    spans = -(-tokens // LANES)
    peers = all_ref.shape[0] // (8 * spans)
    spread = []
    for q in range(spans):
        cross, mass, highest, sums = (
            all_ref[pl.ds(q * 8 + v, peers, stride=8 * spans), :] for v in range(4)
        )
        top = jnp.max(highest, axis=0, keepdims=True)
        total = jnp.sum(sums * jnp.exp(highest - top), axis=0, keepdims=True)
        norm = top + jnp.log(total)
        spread.append(
            jnp.sum(cross, axis=0, keepdims=True) + norm * jnp.sum(mass, axis=0, keepdims=True)
        )
    kl = jnp.concatenate(spread, axis=1)
    mask = mask_ref[...]
    counted = jnp.sum(mask.astype(F32), axis=1, keepdims=True)
    width = kl.shape[1]
    place = iota((1, width), 1)
    kl = jnp.where((place < rows) & ((place + first).astype(F32) < counted), kl, 0.0)
    row = iota((16, width), 0)
    parts = jnp.zeros((16, width), F32)
    for v, part in enumerate(thirds(kl)):
        parts = jnp.where(row == v, jnp.broadcast_to(part, (16, width)), parts)
    back = jnp.dot(parts.astype(BF16), selector(mask, width, first), preferred_element_type=F32)
    loss = jnp.sum(back, axis=0, keepdims=True) * mask.astype(F32)
    loss_ref[...] = loss
    lane = iota((8, LANES), 1)
    sums_ref[...] = jnp.where(
        lane == 0, jnp.sum(loss, axis=1, keepdims=True), jnp.where(lane == 1, counted, 0.0)
    )


def whole(memory_space):
    return pl.BlockSpec(memory_space=memory_space)


VM, SM, HB = pltpu.VMEM, pltpu.SMEM, pl.ANY


def exchanged(teacher_logits, student_logits, dest, tile_weight, mask, rows, first):
    peers = lax.axis_size("vocab")
    me = lax.axis_index("vocab").astype(jnp.int32).reshape(1)
    tokens = teacher_logits.shape[0]
    tb_dev = teacher_logits.shape[1] // BLOCK
    sb_dev = student_logits.shape[1] // BLOCK
    wide = -(-tokens // LANES) * LANES
    stat_rows = wide // LANES * STAT_ROWS
    tiles = tb_dev * K
    dma = pltpu.SemaphoreType.DMA
    send = pl.pallas_call(
        functools.partial(send_kernel, rows, first, sb_dev),
        out_shape=jax.ShapeDtypeStruct((peers, CAP * rows + stat_rows, LANES), BF16),
        in_specs=[whole(SM), whole(SM), whole(VM), whole(HB), whole(HB)],
        out_specs=whole(HB),
        scratch_shapes=[
            VM(teacher_logits.shape, BF16),
            VM(tile_weight.shape, BF16),
            VM((rows, tokens), BF16),
            VM((rows, tb_dev * BLOCK), BF16),
            VM((tb_dev, BLOCK, K * BLOCK), BF16),
            VM((tiles, rows, BLOCK), BF16),
            VM((wide, LANES), F32),
            VM((stat_rows, LANES), BF16),
            VM((rows, LANES), F32),
            VM((rows, LANES), F32),
            SM((peers,), jnp.int32),
            dma(()),
            dma((4,)),
            dma((tiles,)),
            dma((peers,)),
        ],
        compiler_params=pltpu.CompilerParams(vmem_limit_bytes=48 << 20),
        name="send",
    )(me, dest, mask, teacher_logits, tile_weight)
    received = lax.all_to_all(send, "vocab", 0, 0, tiled=True)
    kept, s_stat, counts, slots = pl.pallas_call(
        functools.partial(student_kernel, rows, first, peers, tb_dev),
        out_shape=(
            jax.ShapeDtypeStruct((rows, student_logits.shape[1]), BF16),
            jax.ShapeDtypeStruct((8, wide), F32),
            jax.ShapeDtypeStruct((sb_dev + 1,), jnp.int32),
            jax.ShapeDtypeStruct((sb_dev * peers * CAP,), jnp.int32),
        ),
        in_specs=[whole(SM), whole(SM), whole(VM), whole(HB)],
        out_specs=(whole(VM), whole(VM), whole(SM), whole(SM)),
        scratch_shapes=[
            VM(student_logits.shape, BF16),
            VM((rows, tokens), BF16),
            VM((wide, LANES), F32),
            VM((rows, LANES), F32),
            dma((2,)),
        ],
        compiler_params=pltpu.CompilerParams(vmem_limit_bytes=32 << 20),
        cost_estimate=pl.CostEstimate(
            flops=40 * 10**9, bytes_accessed=6 * 10**6, transcendentals=2 * 10**6
        ),
        name="student",
    )(me, dest, mask, student_logits)
    chunk = rows // 4 if rows % 64 == 0 else rows
    mine = pl.pallas_call(
        functools.partial(combine_kernel, rows, chunk),
        out_shape=jax.ShapeDtypeStruct((peers * 8 * (wide // LANES), LANES), F32),
        in_specs=[whole(SM), whole(SM), whole(HB), whole(VM), whole(VM)],
        out_specs=whole(VM),
        scratch_shapes=[
            VM((CAP, peers, rows, LANES), BF16),
            VM((peers, stat_rows, LANES), BF16),
            VM((peers * stat_rows, LANES), F32),
            VM((wide, LANES), F32),
            VM((peers, chunk, LANES), F32),
            VM((wide, LANES), F32),
            dma((rows // chunk, CAP)),
            dma(()),
        ],
        compiler_params=pltpu.CompilerParams(vmem_limit_bytes=40 << 20),
        name="combine",
    )(counts, slots, received, kept, s_stat)
    everyone = lax.all_to_all(mine, "vocab", 0, 0, tiled=True)
    return pl.pallas_call(
        functools.partial(loss_kernel, rows, first),
        out_shape=(
            jax.ShapeDtypeStruct((1, tokens), F32),
            jax.ShapeDtypeStruct((8, LANES), F32),
        ),
        in_specs=[whole(VM), whole(VM)],
        out_specs=(whole(VM), whole(VM)),
        name="loss",
    )(everyone, mask)


def summed_over(x, axis):
    size = lax.axis_size(axis)
    terms = [x] + [
        lax.ppermute(x, axis, [(i, i ^ flip) for i in range(size)]) for flip in range(1, size)
    ]
    while len(terms) > 1:
        terms = [a + b for a, b in zip(terms[::2], terms[1::2])]
    return terms[0]


def local(teacher_logits, student_logits, tile_dest, tile_weight, token_mask):
    tokens = teacher_logits.shape[0]
    loss, sums = exchanged(
        teacher_logits, student_logits, tile_dest.T, tile_weight, token_mask.reshape(1, tokens),
        tokens, 0,
    )
    total = summed_over(sums[0:1], "dp")
    return loss.reshape(tokens), total[0, 0] / total[0, 1]


def solution(mesh):
    in_specs = (P("dp", "vocab"), P("dp", "vocab"), P(), P("vocab", None, None, None), P("dp"))
    out_specs = (P("dp"), P())
    return jax.shard_map(local, mesh=mesh, in_specs=in_specs, out_specs=out_specs, check_vma=False)
```

time: 260 us -> 214 us (0.82)
  Pallas kernels: 0 us -> 70.1 us
  blocking collectives: 90.8 us -> 21.3 us
  local copies, waits for them, and re-layouts: 48.1 us -> 8.21 us
  waiting for transfers between devices: 54 us -> 82.5 us
  matrix products: 25.9 us -> 0 us
  other arithmetic: 19.3 us -> 1.92 us
  starting transfers between devices: 17.1 us -> 23.6 us
    pallas_call x0 -> x4, Pallas kernels: none -> 70.1 us  [the longest x1 33.1 us: exchanged(): pl.pallas_call(functools.partial(student_kernel, rows, first, peers, tb_d...]
    all_to_all x3 -> x1, blocking collectives: 90.8 us -> 21.3 us  [exchanged(): everyone = lax.all_to_all(mine, 'vocab', 0, 0, tiled=True)]
    all_to_all x3 -> x1, waiting for transfers between devices: 54 us -> 82.2 us  [exchanged(): received = lax.all_to_all(send, 'vocab', 0, 0, tiled=True)]
    dot_general x5 -> x0, matrix products: 25.9 us -> none  [the longest x2 10.9 us: collect(): jnp.einsum('snd,sj->njd', flat_items, slot_table, preferred_element_type=...]
    ppermute x0 -> x7, starting transfers between devices: none -> 14.9 us  [summed_over(): lax.ppermute(x, axis, [(i, i ^ flip) for i in range(size)])]
    convert_element_type x1 -> x0, local copies, waits for them, and re-layouts: 11 us -> none  [local(): outgoing.astype(jnp.bfloat16).reshape(group_size, capacity, tok_rows, BLOCK)]
    reduce_sum x6 -> x0, other arithmetic: 10.4 us -> none  [the longest x1 3.95 us: local(): cross_part = jnp.sum(target * (jnp.log(target) - student_vals), axis=1)]
    reshape x6 -> x1, local copies, waits for them, and re-layouts: 10.8 us -> 0.68 us  [local(): token_mask.reshape(1, tokens)]
  transfers between devices with their start and end apart: 3 -> 8, of which waited for: 3 -> 2; matrix products, arithmetic and copies ran while one was open for 6% -> 1% of each run, Pallas kernels for 0% -> 16%
where the time goes in v1:
time: 214 us; the launch traced here: 211 us
  waiting for transfers between devices  82.5 us (39%)
  Pallas kernels  70.1 us (33%)
  starting transfers between devices  23.6 us (11%)
  blocking collectives  21.3 us (10%)
  local copies, waits for them, and re-layouts  8.21 us (4%)
  between operations  3.16 us (1%)
    all_to_all x1, waiting for transfers between devices, exchanged(): received = lax.all_to_all(send, 'vocab', 0, 0, tiled=True)  82.2 us
    pallas_call x1, Pallas kernels, exchanged(): pl.pallas_call(functools.partial(student_kernel, rows, first, peers, tb_d...  33.1 us
    all_to_all x1, blocking collectives, exchanged(): everyone = lax.all_to_all(mine, 'vocab', 0, 0, tiled=True)  21.3 us
    pallas_call x1, Pallas kernels, exchanged(): pl.pallas_call(functools.partial(send_kernel, rows, first, sb_dev), out_s...  20.1 us
    pallas_call x1, Pallas kernels, exchanged(): pl.pallas_call(functools.partial(combine_kernel, rows, chunk), out_shape=...  15 us
    ppermute x7, starting transfers between devices, summed_over(): lax.ppermute(x, axis, [(i, i ^ flip) for i in range(size)])  14.9 us
    all_to_all x1, starting transfers between devices, exchanged(): received = lax.all_to_all(send, 'vocab', 0, 0, tiled=True)  8.65 us
    unnamed x12, local copies, waits for them, and re-layouts  6.28 us
  transfers between devices with their start and end apart: 8, of which 2 were waited for; matrix products, arithmetic and copies ran while one was open for 1% of the time, Pallas kernels for 16%

profile of v1, /device:TPU:1, one launch (start us, length us, event | category | flops | bytes accessed | tf_op | source)
XLA Modules:
  0.0 210.8 jit_solution(12331299536858039386)
XLA Ops:
  0.6 0.7 reshape.17.mask_ref
  1.3 2.0 copy-done
  3.4 1.7 copy-done.1
  5.0 0.7 copy-done.3
  5.7 20.1 %send.1 = bf16[32,1200,128]{2,1,0:T(8,128)(2,1)} custom-call(s32[1]{0:T(128)} %bitcast.me_ref, s32[2,1184]{1,0:T(2,128)S(1)} %bitcast.6, s32[1,384]{1,0:T(1,128)S(1)} %reshape.17.mask_ref, bf16[384,4736]{1,0:T(8,128)(2,1)S(1)} %copy-done, bf16[37,2,128,128]{3,2,1,0:T(8,128)(2,1)S(1)} %copy-done.1), custom_call_target="tpu_custom_call" | custom-call | tf_op jit(solution)/shard_map/send/pallas_call | solution.py:345
  25.8 0.0 copy-start.4
  25.9 8.6 %all-to-all-start = ((bf16[32,1200,128]{2,1,0:T(8,128)(2,1)}), bf16[32,1200,128]{2,1,0:T(8,128)(2,1)}, u32[]{:S(2)}, u32[]{:S(2)}) async-start(bf16[32,1200,128]{2,1,0:T(8,128)(2,1)} %send.1), calls=%async_computation | async-start | bytes 19660800 | tf_op jit(solution)/shard_map/all_to_all | solution.py:370
  34.5 1.9 copy-done.5
  36.4 33.1 %student.1 = (bf16[384,3968]{1,0:T(8,128)(2,1)S(1)}, f32[8,384]{1,0:T(8,128)S(1)}, s32[32]{0:T(128)S(1)}, s32[2976]{0:T(1024)S(1)}) custom-call(s32[1]{0:T(128)} %bitcast.me_ref, s32[2,1184]{1,0:T(2,128)S(1)} %bitcast.7, s32[1,384]{1,0:T(1,128)S(1)} %reshape.17.mask_ref, bf16[384,3968]{1,0:T(8,128)(2,1)S(1)} %copy-done.5), custom_call_target="tpu_custom_call" | custom-call | flops 40000000000 | bytes 6000000 | tf_op jit(solution)/shard_map/student/pallas_call | solution.py:371
  69.5 82.2 %all-to-all-done.recv_hbm = bf16[32,1200,128]{2,1,0:T(8,128)(2,1)} async-done(((bf16[32,1200,128]{2,1,0:T(8,128)(2,1)}), bf16[32,1200,128]{2,1,0:T(8,128)(2,1)}, u32[]{:S(2)}, u32[]{:S(2)}) %all-to-all-start) | async-done | bytes 9830432 | tf_op jit(solution)/shard_map/all_to_all | solution.py:370
  151.7 15.0 %combine.1 = f32[768,128]{1,0:T(8,128)S(1)} custom-call(s32[32]{0:T(128)S(1)} %get-tuple-element.8.count_ref, s32[2976]{0:T(1024)S(1)} %get-tuple-element.9.slot_ref, bf16[32,1200,128]{2,1,0:T(8,128)(2,1)} %all-to-all-done.recv_hbm, bf16[384,3968]{1,0:T(8,128)(2,1)S(1)} %get-tuple-element.10.s_ref, f32[8,384]{1,0:T(8,128)S(1)} %get-tuple-element.11.s_stat_ref), custom_call_target="tpu_custom_call" | custom-call | tf_op jit(solution)/shard_map/combine/pallas_call | solution.py:395
  166.7 21.3 %all_to_all.16 = f32[32,24,128]{2,1,0:T(8,128)} all-to-all(f32[32,24,128]{2,1,0:T(8,128)S(1)} %bitcast.5), channel_id=1, replica_groups=mesh['dp'=8,'vocab'=32] {'vocab'}, dimensions={0} | all-to-all | bytes 786432 | tf_op jit(solution)/shard_map/all_to_all | solution.py:413
  188.0 2.0 loss.1
  190.0 0.7 slice.9
  190.6 6.0 %collective-permute-start.5 = (f32[1,128]{1,0:T(1,128)S(1)}, f32[1,128]{1,0:T(1,128)S(1)}, u32[]{:S(2)}, u32[]{:S(2)}) collective-permute-start(f32[1,128]{1,0:T(1,128)S(1)} %slice.9), channel_id=1, source_target_pairs={{0,192},{32,224},{64,128},{96,160},{128,64},{160,96},{192,0},{224,... | collective-permute-start | bytes 1544 | tf_op jit(solution)/shard_map/ppermute | solution.py:429
  196.7 0.7 collective-permute-start.4
  197.4 4.2 %collective-permute-start.3 = (f32[1,128]{1,0:T(1,128)S(1)}, f32[1,128]{1,0:T(1,128)S(1)}, u32[]{:S(2)}, u32[]{:S(2)}) collective-permute-start(f32[1,128]{1,0:T(1,128)S(1)} %slice.9), channel_id=1, source_target_pairs={{0,128},{32,160},{64,192},{96,224},{128,0},{160,32},{192,64},{224,... | collective-permute-start | bytes 1544 | tf_op jit(solution)/shard_map/ppermute | solution.py:429
  201.6 1.6 collective-permute-start.2
  203.2 0.3 collective-permute-start.1
  203.5 2.1 collective-permute-start
  205.6 1.3 reduce
  206.9 0.2 collective-permute-done.6
  207.1 0.7 add_add_fusion
  207.8 0.6 fusion
  (14 shorter events, 0.0 us)
Async XLA Ops:
  1.3 33.2 %copy-start.2 = (s32[1,384]{1,0:T(1,128)}, s32[1,384]{1,0:T(1,128)S(1)}, u32[]{:S(2)}) copy-start(s32[1,384]{1,0:T(1,128)S(1)} %reshape.17.mask_ref) | copy-start | bytes 4612
  1.3 2.0 copy-start
  3.4 1.7 copy-start.1
  5.0 0.7 copy-start.3
  25.8 8.7 %copy-start.4 = (s32[1184,2]{0,1:T(2,128)S(1)}, s32[1184,2]{0,1:T(2,128)}, u32[]{:S(2)}) copy-start(s32[1184,2]{0,1:T(2,128)} %param.7) | copy-start | bytes 28420
  25.9 125.8 %all-to-all-start = ((bf16[32,1200,128]{2,1,0:T(8,128)(2,1)}), bf16[32,1200,128]{2,1,0:T(8,128)(2,1)}, u32[]{:S(2)}, u32[]{:S(2)}) async-start(bf16[32,1200,128]{2,1,0:T(8,128)(2,1)} %send.1), calls=%async_computation | async-start | bytes 19660800 | tf_op jit(solution)/shard_map/all_to_all | solution.py:370
  34.5 1.9 copy-start.5
  190.6 12.9 %collective-permute-start.5 = (f32[1,128]{1,0:T(1,128)S(1)}, f32[1,128]{1,0:T(1,128)S(1)}, u32[]{:S(2)}, u32[]{:S(2)}) collective-permute-start(f32[1,128]{1,0:T(1,128)S(1)} %slice.9), channel_id=1, source_target_pairs={{0,192},{32,224},{64,128},{96,160},{128,64},{160,96},{192,0},{224,... | collective-permute-start | bytes 1544 | tf_op jit(solution)/shard_map/ppermute | solution.py:429
  196.7 6.8 %collective-permute-start.4 = (f32[1,128]{1,0:T(1,128)S(1)}, f32[1,128]{1,0:T(1,128)S(1)}, u32[]{:S(2)}, u32[]{:S(2)}) collective-permute-start(f32[1,128]{1,0:T(1,128)S(1)} %slice.9), channel_id=1, source_target_pairs={{0,160},{32,128},{64,224},{96,192},{128,32},{160,0},{192,96},{224,... | collective-permute-start | bytes 1544 | tf_op jit(solution)/shard_map/ppermute | solution.py:429
  197.4 9.5 %collective-permute-start.3 = (f32[1,128]{1,0:T(1,128)S(1)}, f32[1,128]{1,0:T(1,128)S(1)}, u32[]{:S(2)}, u32[]{:S(2)}) collective-permute-start(f32[1,128]{1,0:T(1,128)S(1)} %slice.9), channel_id=1, source_target_pairs={{0,128},{32,160},{64,192},{96,224},{128,0},{160,32},{192,64},{224,... | collective-permute-start | bytes 1544 | tf_op jit(solution)/shard_map/ppermute | solution.py:429
  201.6 5.3 %collective-permute-start.2 = (f32[1,128]{1,0:T(1,128)S(1)}, f32[1,128]{1,0:T(1,128)S(1)}, u32[]{:S(2)}, u32[]{:S(2)}) collective-permute-start(f32[1,128]{1,0:T(1,128)S(1)} %slice.9), channel_id=1, source_target_pairs={{0,96},{32,64},{64,32},{96,0},{128,224},{160,192},{192,160},{224,1... | collective-permute-start | bytes 1544 | tf_op jit(solution)/shard_map/ppermute | solution.py:429
  203.2 3.6 %collective-permute-start.1 = (f32[1,128]{1,0:T(1,128)S(1)}, f32[1,128]{1,0:T(1,128)S(1)}, u32[]{:S(2)}, u32[]{:S(2)}) collective-permute-start(f32[1,128]{1,0:T(1,128)S(1)} %slice.9), channel_id=1, source_target_pairs={{0,64},{32,96},{64,0},{96,32},{128,192},{160,224},{192,128},{224,1... | collective-permute-start | bytes 1544 | tf_op jit(solution)/shard_map/ppermute | solution.py:429
  203.5 3.6 %collective-permute-start.6 = (f32[1,128]{1,0:T(1,128)S(1)}, f32[1,128]{1,0:T(1,128)S(1)}, u32[]{:S(2)}, u32[]{:S(2)}) collective-permute-start(f32[1,128]{1,0:T(1,128)S(1)} %slice.9), channel_id=1, source_target_pairs={{0,224},{32,192},{64,160},{96,128},{128,96},{160,64},{192,32},{224... | collective-permute-start | bytes 1544 | tf_op jit(solution)/shard_map/ppermute | solution.py:429
  203.5 3.6 %collective-permute-start = (f32[1,128]{1,0:T(1,128)S(1)}, f32[1,128]{1,0:T(1,128)S(1)}, u32[]{:S(2)}, u32[]{:S(2)}) collective-permute-start(f32[1,128]{1,0:T(1,128)S(1)} %slice.9), channel_id=1, source_target_pairs={{0,32},{32,0},{64,96},{96,64},{128,160},{160,128},{192,224},{224,1... | collective-permute-start | bytes 1544 | tf_op jit(solution)/shard_map/ppermute | solution.py:429

commit v2 on v1

v2 whole, which is shorter than its diff:
```python
import functools

import jax
import jax.numpy as jnp
from jax import lax
from jax.experimental import pallas as pl
from jax.experimental.pallas import tpu as pltpu
from jax.sharding import PartitionSpec as P

BLOCK = 128
VS = 126976
K = 2
CAP = 3
SMOOTH = 0.1
LANES = 128
GROUP = 4
FACTS = 32
ROUTE = 24
F32 = jnp.float32
BF16 = jnp.bfloat16


def iota(shape, dim):
    return lax.broadcasted_iota(jnp.int32, shape, dim)


def selector(mask_row, rows, first):
    tokens = mask_row.shape[1]
    before = (iota((tokens, tokens), 0) < iota((tokens, tokens), 1)).astype(F32).astype(BF16)
    kept = jnp.broadcast_to(mask_row.astype(F32), (16, tokens)).astype(BF16)
    rank = jnp.dot(kept, before, preferred_element_type=F32)[0:1]
    wanted = (iota((rows, tokens), 0) + first).astype(F32)
    hit = (wanted == jnp.broadcast_to(rank, (rows, tokens))) & (
        jnp.broadcast_to(mask_row, (rows, tokens)) > 0
    )
    return hit.astype(F32).astype(BF16)


def thirds(value):
    high = value.astype(BF16).astype(F32)
    middle = (value - high).astype(BF16).astype(F32)
    low = (value - high - middle).astype(BF16).astype(F32)
    return high, middle, low


def in_lanes(columns, rows):
    lane = iota((rows, LANES), 1)
    out = jnp.zeros((rows, LANES), F32)
    for v, column in enumerate(columns):
        out = jnp.where(lane == v, jnp.broadcast_to(column, (rows, LANES)), out)
    return out


def column_copies(hbm, buf, sems, blocks, parts):
    groups = blocks // GROUP
    cuts = [groups * i // parts for i in range(parts + 1)]
    out = []
    for c, (lo, hi) in enumerate(zip(cuts[:-1], cuts[1:])):
        end = hi * GROUP if c < parts - 1 else blocks
        where = (slice(None), pl.ds(lo * GROUP * BLOCK, (end - lo * GROUP) * BLOCK))
        copy = pltpu.make_async_copy(hbm.at[where], buf.at[where], sems.at[c])
        copy.start()
        out.append(((lo, hi), copy))
    return out


def picked(sel_ref, src_ref, dst_ref, top_ref, blocks, copies):
    top_ref[...] = jnp.full(top_ref.shape, -jnp.inf, F32)

    def one(start, count):
        tops = []
        for i in range(0, count, 2):
            width = min(2, count - i) * BLOCK
            at = pl.ds(start + i * BLOCK, width)
            got = jnp.dot(sel_ref[...], src_ref[:, at], preferred_element_type=F32)
            dst_ref[:, at] = got.astype(BF16)
            tops += [got[:, j : j + BLOCK] for j in range(0, width, BLOCK)]
        top_ref[...] = functools.reduce(jnp.maximum, tops, top_ref[...])

    for (lo, hi), copy in copies:
        copy.wait()

        def body(i, carry):
            one(pl.multiple_of(i * GROUP * BLOCK, GROUP * BLOCK), GROUP)
            return carry

        lax.fori_loop(lo, hi, body, 0)
    if blocks % GROUP:
        one(blocks // GROUP * GROUP * BLOCK, blocks % GROUP)


def send_kernel(
    rows, first, sb_dev,
    me_ref, mask_ref, dest_hbm, x_hbm, w_hbm, s_hbm, send_hbm, kept_ref,
    x_buf, w_buf, s_buf, dest, sel, xc, maps, stage, cols, facts, top, total, used,
    in_sem, x_sem, s_sem, out_sem, fact_sem,
):
    blocks = w_buf.shape[0]
    s_blocks = s_buf.shape[1] // BLOCK
    peers = send_hbm.shape[0]
    w_copy = pltpu.make_async_copy(w_hbm, w_buf, in_sem.at[0])
    w_copy.start()
    dest_copy = pltpu.make_async_copy(dest_hbm, dest, in_sem.at[1])
    dest_copy.start()
    x_copies = column_copies(x_hbm, x_buf, x_sem, blocks, 3)
    s_copies = column_copies(s_hbm, s_buf, s_sem, s_blocks, 1)
    sel[...] = selector(mask_ref[...], rows, first)

    def clear(i, carry):
        used[i] = 0
        return carry

    lax.fori_loop(0, peers, clear, 0)
    w_copy.wait()
    ones = jnp.ones((K * BLOCK, BLOCK), BF16)

    def weight(b):
        both = jnp.concatenate([w_buf[b, k] for k in range(K)], axis=1)
        scale = 1.0 / jnp.dot(both, ones, preferred_element_type=F32)
        maps[b] = (both.astype(F32) * jnp.concatenate([scale] * K, axis=1)).astype(BF16)

    def weights(i, carry):
        for j in range(GROUP):
            weight(i * GROUP + j)
        return carry

    lax.fori_loop(0, blocks // GROUP, weights, 0)
    for b in range(blocks // GROUP * GROUP, blocks):
        weight(b)
    picked(sel, x_buf, xc, top, blocks, x_copies)
    highest = jnp.max(top[...], axis=1, keepdims=True)
    top[...] = jnp.broadcast_to(highest, top.shape)
    total[...] = jnp.zeros(total.shape, F32)
    dest_copy.wait()
    base = me_ref[0] * blocks
    top_block = peers * sb_dev
    factor = (1 << 16) // sb_dev + 1
    assert all(d * factor >> 16 == d // sb_dev for d in range(top_block))
    lane = iota((8, LANES), 1)

    def raised(b):
        at = pl.ds(pl.multiple_of(b * BLOCK, BLOCK), BLOCK)
        return jnp.exp(xc[:, at].astype(F32) - top[...])

    def tile(b, value, route):
        mapped = jnp.dot(value.astype(BF16), maps[b], preferred_element_type=F32)
        for k in range(K):
            stage[K * b + k] = mapped[:, k * BLOCK : (k + 1) * BLOCK].astype(BF16)
            block = dest[k, base + b]
            owner = lax.shift_right_logical(block * factor, 16)
            rank = used[owner]
            used[owner] = rank + 1
            near = (block - owner * sb_dev).astype(F32)
            route = jnp.where(lane == owner * CAP + rank, near, route)
            pltpu.make_async_copy(
                stage.at[K * b + k],
                send_hbm.at[owner, pl.ds(pl.multiple_of(rank * rows, 16), rows)],
                out_sem.at[K * b + k],
            ).start()
        return route

    def pair(i, route):
        one, two = raised(2 * i), raised(2 * i + 1)
        total[...] += one + two
        return tile(2 * i + 1, two, tile(2 * i, one, route))

    route = lax.fori_loop(0, blocks // 2, pair, jnp.full((8, LANES), sb_dev, F32))
    if blocks % 2:
        last = raised(blocks - 1)
        total[...] += last
        route = tile(blocks - 1, last, route)
    summed = jnp.sum(total[...], axis=1, keepdims=True)
    cols[...] = jnp.zeros(cols.shape, F32)

    picked(sel, s_buf, kept_ref, top, s_blocks, s_copies)
    s_highest = jnp.max(top[...], axis=1, keepdims=True)
    top[...] = jnp.broadcast_to(s_highest, top.shape)
    total[...] = jnp.zeros(total.shape, F32)

    def student(start, count):
        at = [pl.ds(start + i * BLOCK, BLOCK) for i in range(count)]
        total[...] += sum(jnp.exp(kept_ref[:, a].astype(F32) - top[...]) for a in at)

    def students(i, carry):
        student(pl.multiple_of(i * GROUP * BLOCK, GROUP * BLOCK), GROUP)
        return carry

    lax.fori_loop(0, s_blocks // GROUP, students, 0)
    if s_blocks % GROUP:
        student(s_blocks // GROUP * GROUP * BLOCK, s_blocks % GROUP)
    s_summed = jnp.sum(total[...], axis=1, keepdims=True)
    cols[0:rows] = in_lanes((highest, *thirds(summed), s_highest, *thirds(s_summed)), rows)
    for q in range(ROUTE // 8):
        if q < cols.shape[0] // LANES:
            turned = cols[q * LANES : (q + 1) * LANES].T
            total[q * 8 : (q + 1) * 8] = turned[:8]
        else:
            total[q * 8 : (q + 1) * 8] = jnp.zeros((8, LANES), F32)
    total[ROUTE : ROUTE + 8] = route
    facts[...] = total[0:FACTS].astype(BF16)

    def fact_copy(d):
        return pltpu.make_async_copy(
            facts, send_hbm.at[d, pl.ds(CAP * rows, FACTS)], fact_sem.at[d]
        )

    def fact_start(d, carry):
        fact_copy(d).start()
        return carry

    def fact_wait(d, carry):
        fact_copy(d).wait()
        return carry

    def tile_wait(i, carry):
        pltpu.make_async_copy(
            stage.at[i], send_hbm.at[0, pl.ds(0, rows)], out_sem.at[i]
        ).wait()
        return carry

    lax.fori_loop(0, peers, fact_start, 0)
    lax.fori_loop(0, K * blocks, tile_wait, 0)
    lax.fori_loop(0, peers, fact_wait, 0)


def combine_kernel(
    rows, first, chunk, everyone,
    me_ref, mask_ref, recv_hbm, s_ref, out_ref,
    buf, facts, facts32, share, near_vm, near, acc, cols, sems, fact_sem, near_sem,
):
    peers = recv_hbm.shape[0]
    blocks = s_ref.shape[1] // BLOCK
    spans = -(-rows // LANES)
    fact_copy = pltpu.make_async_copy(
        recv_hbm.at[:, pl.ds(CAP * rows, FACTS)], facts, fact_sem
    )
    fact_copy.start()

    def piece_copy(q, r):
        start = pl.multiple_of(q * chunk, chunk)
        return pltpu.make_async_copy(
            recv_hbm.at[:, pl.ds(r * rows + start, chunk)],
            buf.at[r, :, pl.ds(start, chunk)],
            sems.at[q, r],
        )

    for q in range(rows // chunk):
        for r in range(CAP):
            piece_copy(q, r).start()
    fact_copy.wait()
    facts32[...] = facts[...].astype(F32).reshape(facts32.shape)

    def fact(row):
        return facts32[pl.ds(row, peers, stride=FACTS), :]

    lane = iota((peers, LANES), 1)
    routes = fact(ROUTE)
    slots = jnp.zeros((peers, LANES), F32)
    for r in range(CAP):
        mine = jnp.where(lane == me_ref[0] * CAP + r, routes, 0.0)
        slots = jnp.where(lane == r, jnp.sum(mine, axis=1, keepdims=True), slots)
    near_vm[...] = slots.astype(jnp.int32)
    near_copy = pltpu.make_async_copy(near_vm, near, near_sem)
    near_copy.start()
    for q in range(spans):
        highest, high, middle, low, s_highest, s_high, s_middle, s_low = (
            fact(q * 8 + v) for v in range(8)
        )
        raised = jnp.exp(highest - jnp.max(highest, axis=0, keepdims=True))
        total = jnp.sum(raised * ((high + middle) + low), axis=0, keepdims=True)
        part = raised * ((1.0 - SMOOTH) / total)
        s_top = jnp.max(s_highest, axis=0, keepdims=True)
        s_total = jnp.sum(
            jnp.exp(s_highest - s_top) * ((s_high + s_middle) + s_low), axis=0, keepdims=True
        )
        norm = jnp.broadcast_to(s_top + jnp.log(s_total), (LANES - peers, LANES))
        share[q * LANES : (q + 1) * LANES] = jnp.concatenate([part, norm], axis=0).T
    cols[...] = jnp.zeros(cols.shape, F32)
    near_copy.wait()

    def work(q, carry):
        at = pl.ds(pl.multiple_of(q * chunk, chunk), chunk)
        shares = share[at]
        acc[...] = jnp.zeros(acc.shape, F32)
        for r in range(CAP):
            piece_copy(q, r).wait()
        for source in range(peers):
            scale = jnp.broadcast_to(shares[:, source : source + 1], (chunk, LANES))
            for r in range(CAP):
                acc[near[source, r]] += scale * buf[r, source, at].astype(F32)
        norm = jnp.broadcast_to(shares[:, peers : peers + 1], (chunk, LANES))

        def block(j, cross):
            target = acc[j] + SMOOTH / VS
            student = s_ref[at, pl.ds(pl.multiple_of(j * BLOCK, BLOCK), BLOCK)].astype(F32)
            return cross + target * (jnp.log(target) - (student - norm))

        cross = lax.fori_loop(0, blocks, block, jnp.zeros((chunk, LANES), F32))
        cols[at] = jnp.broadcast_to(jnp.sum(cross, axis=1, keepdims=True), (chunk, LANES))
        return carry

    lax.fori_loop(0, rows // chunk, work, 0)
    counted = jnp.sum(mask_ref[...].astype(F32), axis=1, keepdims=True)
    row = iota((8, LANES), 0)
    place = iota((8, LANES), 1)
    values = jnp.zeros((8, LANES), F32)
    part = jnp.zeros((8, LANES), F32)
    for q in range(spans):
        kl = cols[q * LANES : (q + 1) * LANES].T[:8]
        ahead = place + q * LANES
        kl = jnp.where((ahead < rows) & ((ahead + first).astype(F32) < counted), kl, 0.0)
        values = jnp.where(row % 4 == q, kl, values)
        part = part + kl
    whole_sum = jnp.broadcast_to(jnp.sum(part, axis=1, keepdims=True), (8, LANES))
    tally = jnp.where(place == 0, whole_sum, jnp.where(place == 1, counted, 0.0))
    values = jnp.where(row % 4 == 3, tally, values)
    for d in range(everyone // 2):
        out_ref[d * 8 : (d + 1) * 8] = values


def loss_kernel(rows, first, peers, group_ref, all_ref, mask_ref, loss_ref, sums_ref):
    everyone = all_ref.shape[0] // 4
    spans = -(-rows // LANES)
    base = group_ref[0] * (peers * 4)
    kl = jnp.concatenate(
        [
            jnp.sum(all_ref[pl.ds(base + q, peers, stride=4), :], axis=0, keepdims=True)
            for q in range(spans)
        ],
        axis=1,
    )
    mask = mask_ref[...]
    width = spans * LANES
    row = iota((16, width), 0)
    parts = jnp.zeros((16, width), F32)
    for v, part in enumerate(thirds(kl)):
        parts = jnp.where(row == v, jnp.broadcast_to(part, (16, width)), parts)
    back = jnp.dot(parts.astype(BF16), selector(mask, width, first), preferred_element_type=F32)
    loss_ref[...] = jnp.sum(back, axis=0, keepdims=True) * mask.astype(F32)
    tallies = all_ref[pl.ds(3, everyone, stride=4), :]
    lane = iota((1, LANES), 1)
    sums = jnp.sum(tallies, axis=0, keepdims=True)
    most = jnp.max(tallies, axis=0, keepdims=True)
    sums = jnp.where(lane == 1, sums * (1.0 / peers), sums)
    most = jnp.where(lane == 1, most, 0.0)
    row = iota((8, LANES), 0)
    sums_ref[...] = jnp.where(
        row == 0, jnp.broadcast_to(sums, (8, LANES)), jnp.broadcast_to(most, (8, LANES))
    )


def whole(memory_space):
    return pl.BlockSpec(memory_space=memory_space)


VM, SM, HB = pltpu.VMEM, pltpu.SMEM, pltpu.HBM


def exchanged(teacher_logits, student_logits, dest, tile_weight, mask, rows, first):
    peers = lax.axis_size("vocab")
    everyone = peers * lax.axis_size("dp")
    me = lax.axis_index("vocab").astype(jnp.int32).reshape(1)
    group = lax.axis_index("dp").astype(jnp.int32).reshape(1)
    tokens = teacher_logits.shape[0]
    tb_dev = teacher_logits.shape[1] // BLOCK
    sb_dev = student_logits.shape[1] // BLOCK
    wide = -(-rows // LANES) * LANES
    tiles = tb_dev * K
    dma = pltpu.SemaphoreType.DMA
    tall = max(rows, LANES)
    send, kept = pl.pallas_call(
        functools.partial(send_kernel, rows, first, sb_dev),
        out_shape=(
            jax.ShapeDtypeStruct((peers, CAP * rows + FACTS, LANES), BF16),
            jax.ShapeDtypeStruct((rows, student_logits.shape[1]), BF16),
        ),
        in_specs=[whole(SM), whole(VM), whole(HB), whole(HB), whole(HB), whole(HB)],
        out_specs=(whole(HB), whole(VM)),
        scratch_shapes=[
            VM(teacher_logits.shape, BF16),
            VM(tile_weight.shape, BF16),
            VM(student_logits.shape, BF16),
            SM(dest.shape, jnp.int32),
            VM((rows, tokens), BF16),
            VM((rows, tb_dev * BLOCK), BF16),
            VM((tb_dev, BLOCK, K * BLOCK), BF16),
            VM((tiles, rows, BLOCK), BF16),
            VM((wide, LANES), F32),
            VM((FACTS, LANES), BF16),
            VM((rows, LANES), F32),
            VM((rows, LANES), F32),
            SM((peers,), jnp.int32),
            dma((2,)),
            dma((3,)),
            dma((1,)),
            dma((tiles,)),
            dma((peers,)),
        ],
        compiler_params=pltpu.CompilerParams(vmem_limit_bytes=56 << 20),
        name="send",
    )(me, mask, dest, teacher_logits, tile_weight, student_logits)
    received = lax.all_to_all(send, "vocab", 0, 0, tiled=True)
    chunk = rows // 4 if rows % 64 == 0 else rows
    mine = pl.pallas_call(
        functools.partial(combine_kernel, rows, first, chunk, everyone),
        out_shape=jax.ShapeDtypeStruct((everyone * 4, LANES), F32),
        in_specs=[whole(SM), whole(VM), whole(HB), whole(VM)],
        out_specs=whole(VM),
        scratch_shapes=[
            VM((CAP, peers, rows, LANES), BF16),
            VM((peers, FACTS, LANES), BF16),
            VM((peers * FACTS, LANES), F32),
            VM((wide, LANES), F32),
            VM((peers, LANES), jnp.int32),
            SM((peers, LANES), jnp.int32),
            VM((sb_dev + 1, chunk, LANES), F32),
            VM((wide, LANES), F32),
            dma((rows // chunk, CAP)),
            dma(()),
            dma(()),
        ],
        compiler_params=pltpu.CompilerParams(vmem_limit_bytes=40 << 20),
        name="combine",
    )(me, mask, received, kept)
    collected = lax.all_to_all(mine, ("dp", "vocab"), 0, 0, tiled=True)
    return pl.pallas_call(
        functools.partial(loss_kernel, rows, first, peers),
        out_shape=(
            jax.ShapeDtypeStruct((1, tokens), F32),
            jax.ShapeDtypeStruct((8, LANES), F32),
        ),
        in_specs=[whole(SM), whole(VM), whole(VM)],
        out_specs=(whole(VM), whole(VM)),
        name="loss",
    )(group, collected, mask)


def local(teacher_logits, student_logits, tile_dest, tile_weight, token_mask):
    tokens = teacher_logits.shape[0]
    mask = token_mask.reshape(1, tokens)
    parts = (teacher_logits, student_logits, tile_dest.T, tile_weight, mask)
    rows = tokens * 5 // 6 if tokens % 384 == 0 else tokens
    loss, sums = exchanged(*parts, rows, 0)
    total = sums[0, 0]
    if rows < tokens:

        def rest():
            more, more_sums = exchanged(*parts, tokens - rows, rows)
            return loss + more, total + more_sums[0, 0]

        loss, total = lax.cond(sums[1, 1] > rows, rest, lambda: (loss, total))
    return loss.reshape(tokens), total / sums[0, 1]


def solution(mesh):
    in_specs = (P("dp", "vocab"), P("dp", "vocab"), P(), P("vocab", None, None, None), P("dp"))
    out_specs = (P("dp"), P())
    return jax.shard_map(local, mesh=mesh, in_specs=in_specs, out_specs=out_specs, check_vma=False)
```

time: 214 us -> 171 us (0.80); the launches traced: 211 us -> 171 us
  blocking collectives: 21.3 us -> 102 us
  waiting for transfers between devices: 82.5 us -> 19 us
  Pallas kernels: 70.1 us -> 30.8 us
  starting transfers between devices: 23.6 us -> 13.1 us
  local copies, waits for them, and re-layouts: 8.21 us -> 2.07 us
    all_to_all x1, blocking collectives: 21.3 us -> 102 us  [exchanged(): received = lax.all_to_all(send, 'vocab', 0, 0, tiled=True)]
    all_to_all x1, waiting for transfers between devices: 82.2 us -> 19 us  [exchanged(): collected = lax.all_to_all(mine, ('dp', 'vocab'), 0, 0, tiled=True)]
    pallas_call x3 -> x2, Pallas kernels: 50 us -> 10.7 us  [the longest x1 8.85 us: exchanged(): pl.pallas_call(functools.partial(combine_kernel, rows, first, chunk, ever...]
    ppermute x7 -> x0, starting transfers between devices: 14.9 us -> none  [summed_over(): lax.ppermute(x, axis, [(i, i ^ flip) for i in range(size)])]
    unnamed x12 -> x6, local copies, waits for them, and re-layouts: 6.28 us -> 0.01 us
    all_to_all x1, starting transfers between devices: 8.65 us -> 13.1 us  [exchanged(): collected = lax.all_to_all(mine, ('dp', 'vocab'), 0, 0, tiled=True)]
  transfers between devices with their start and end apart: 8 -> 1, of which waited for: 2 -> 1; matrix products, arithmetic and copies ran while one was open for 1% -> 0% of each run, Pallas kernels for 16% -> 0%
where the time goes in v2:
time: 171 us
  blocking collectives  102 us (60%)
  Pallas kernels  30.8 us (18%)
  waiting for transfers between devices  19 us (11%)
  starting transfers between devices  13.1 us (8%)
  between operations  3.74 us (2%)
  local copies, waits for them, and re-layouts  2.07 us (1%)
    all_to_all x1, blocking collectives, exchanged(): received = lax.all_to_all(send, 'vocab', 0, 0, tiled=True)  102 us
    pallas_call x1, Pallas kernels, exchanged(): pl.pallas_call(functools.partial(send_kernel, rows, first, sb_dev), out_s...  20.1 us
    all_to_all x1, waiting for transfers between devices, exchanged(): collected = lax.all_to_all(mine, ('dp', 'vocab'), 0, 0, tiled=True)  19 us
    all_to_all x1, starting transfers between devices, exchanged(): collected = lax.all_to_all(mine, ('dp', 'vocab'), 0, 0, tiled=True)  13.1 us
    pallas_call x1, Pallas kernels, exchanged(): pl.pallas_call(functools.partial(combine_kernel, rows, first, chunk, ever...  8.85 us
  transfers between devices with their start and end apart: 1, of which 1 were waited for; matrix products, arithmetic and copies ran while one was open for 0% of the time, Pallas kernels for 0%

profile of v2, /device:TPU:1, one launch (start us, length us, event | category | flops | bytes accessed | tf_op | source)
XLA Modules:
  0.0 170.9 jit_solution(11147059249333709536)
XLA Ops:
  0.6 0.7 reshape.35.mask_ref
  1.3 20.1 %send.3 = (bf16[32,992,128]{2,1,0:T(8,128)(2,1)}, bf16[320,3968]{1,0:T(8,128)(2,1)}) custom-call(s32[1]{0:T(128)} %bitcast.6.me_ref, s32[1,384]{1,0:T(1,128)S(1)} %reshape.35.mask_ref, s32[2,1184]{1,0:T(2,128)} %bitcast.14, bf16[384,4736]{1,0:T(8,128)(2,1)} %x_hbm.1, bf16[37,2,128,128]{3,2,1,0:T(8,128)(2,1)} %w_hbm.1, bf16[384,3968]{1,0:T(8,128)(2,1)} %s_hbm.1), custom_call_target="tpu_custom_call" | custom-call | tf_op jit(solution)/shard_map/send/pallas_call | solution.py:371
  21.4 0.0 copy-start
  21.4 101.6 %all_to_all.29.recv_hbm = bf16[32,992,128]{2,1,0:T(8,128)(2,1)S(1)} all-to-all(bf16[32,992,128]{2,1,0:T(8,128)(2,1)} %get-tuple-element.42), channel_id=1, replica_groups=mesh['dp'=8,'vocab'=32] {'vocab'}, dimensions={0} | all-to-all | bytes 16252928 | tf_op jit(solution)/shard_map/all_to_all | solution.py:402
  123.0 0.0 copy-done
  123.0 0.0 copy-start.2
  123.0 0.0 copy-start.4
  123.0 8.8 %combine.3 = f32[1024,128]{1,0:T(8,128)} custom-call(s32[1]{0:T(128)} %bitcast.6.me_ref, s32[1,384]{1,0:T(1,128)S(1)} %reshape.35.mask_ref, bf16[32,992,128]{2,1,0:T(8,128)(2,1)S(1)} %all_to_all.29.recv_hbm, bf16[320,3968]{1,0:T(8,128)(2,1)S(1)} %copy-done), custom_call_target="tpu_custom_call" | custom-call | tf_op jit(solution)/shard_map/combine/pallas_call | solution.py:404
  131.9 13.1 %all-to-all-start.3 = ((f32[256,4,128]{2,1,0:T(4,128)}), f32[256,4,128]{2,1,0:T(4,128)}, u32[]{:S(2)}, u32[]{:S(2)}) async-start(f32[256,4,128]{2,1,0:T(4,128)} %bitcast.8), calls=%async_computation.3 | async-start | bytes 1048576 | tf_op jit(solution)/shard_map/all_to_all | solution.py:425
  145.0 19.0 %all-to-all-done.3 = f32[256,4,128]{2,1,0:T(4,128)} async-done(((f32[256,4,128]{2,1,0:T(4,128)}), f32[256,4,128]{2,1,0:T(4,128)}, u32[]{:S(2)}, u32[]{:S(2)}) %all-to-all-start.3) | async-done | bytes 524320 | tf_op jit(solution)/shard_map/all_to_all | solution.py:425
  164.0 1.9 %loss.3 = (f32[1,384]{1,0:T(1,128)S(1)}, f32[8,128]{1,0:T(8,128)}) custom-call(s32[1]{0:T(128)} %bitcast.5.group_ref, f32[1024,128]{1,0:T(8,128)} %bitcast.9.all_ref, s32[1,384]{1,0:T(1,128)S(1)} %reshape.35.mask_ref), custom_call_target="tpu_custom_call" | custom-call | tf_op jit(solution)/shard_map/loss/pallas_call | solution.py:426
  165.8 1.4 fusion
  167.9 0.0 copy-done.2
  167.9 0.0 copy-done.4
  169.1 0.6 reduce
  (1 shorter events, 0.0 us)
Async XLA Ops:
  21.4 101.6 %copy-start = (bf16[320,3968]{1,0:T(8,128)(2,1)S(1)}, bf16[320,3968]{1,0:T(8,128)(2,1)}, u32[]{:S(2)}) copy-start(bf16[320,3968]{1,0:T(8,128)(2,1)} %get-tuple-element.43.s_ref) | copy-start | bytes 7618564
  123.0 44.9 %copy-start.2 = (bf16[384,3968]{1,0:T(8,128)(2,1)S(1)}, bf16[384,3968]{1,0:T(8,128)(2,1)}, u32[]{:S(2)}) copy-start(bf16[384,3968]{1,0:T(8,128)(2,1)} %s_hbm.1) | copy-start | bytes 9142276
  123.0 44.9 %copy-start.4 = (s32[1184,2]{0,1:T(2,128)S(1)}, s32[1184,2]{0,1:T(2,128)}, u32[]{:S(2)}) copy-start(s32[1184,2]{0,1:T(2,128)} %param.9) | copy-start | bytes 28420
  131.9 32.1 %all-to-all-start.3 = ((f32[256,4,128]{2,1,0:T(4,128)}), f32[256,4,128]{2,1,0:T(4,128)}, u32[]{:S(2)}, u32[]{:S(2)}) async-start(f32[256,4,128]{2,1,0:T(4,128)} %bitcast.8), calls=%async_computation.3 | async-start | bytes 1048576 | tf_op jit(solution)/shard_map/all_to_all | solution.py:425

commit v3 on v2

v3 whole, which is shorter than its diff:
```python
import functools

import jax
import jax.numpy as jnp
from jax import lax
from jax.experimental import pallas as pl
from jax.experimental.pallas import tpu as pltpu
from jax.sharding import PartitionSpec as P

BLOCK = 128
VS = 126976
K = 2
CAP = 3
SMOOTH = 0.1
LANES = 128
GROUP = 4
FACTS = 16
ROUTE = 15
VALUES = 6
F32 = jnp.float32
BF16 = jnp.bfloat16


def iota(shape, dim):
    return lax.broadcasted_iota(jnp.int32, shape, dim)


def selector(mask_row, rows, first):
    tokens = mask_row.shape[1]
    before = (iota((tokens, tokens), 0) < iota((tokens, tokens), 1)).astype(F32).astype(BF16)
    kept = jnp.broadcast_to(mask_row.astype(F32), (16, tokens)).astype(BF16)
    rank = jnp.dot(kept, before, preferred_element_type=F32)[0:1]
    wanted = (iota((rows, tokens), 0) + first).astype(F32)
    hit = (wanted == jnp.broadcast_to(rank, (rows, tokens))) & (
        jnp.broadcast_to(mask_row, (rows, tokens)) > 0
    )
    return hit.astype(F32).astype(BF16)


def parted(value, count):
    out = []
    for _ in range(count):
        out.append(value.astype(BF16).astype(F32))
        value = value - out[-1]
    return out


def in_lanes(columns, rows):
    lane = iota((rows, LANES), 1)
    out = jnp.zeros((rows, LANES), F32)
    for v, column in enumerate(columns):
        out = jnp.where(lane == v, jnp.broadcast_to(column, (rows, LANES)), out)
    return out


def column_copies(hbm, buf, sems, blocks, parts):
    groups = blocks // GROUP
    cuts = [groups * i // parts for i in range(parts + 1)]
    out = []
    for c, (lo, hi) in enumerate(zip(cuts[:-1], cuts[1:])):
        end = hi * GROUP if c < parts - 1 else blocks
        where = (slice(None), pl.ds(lo * GROUP * BLOCK, (end - lo * GROUP) * BLOCK))
        copy = pltpu.make_async_copy(hbm.at[where], buf.at[where], sems.at[c])
        copy.start()
        out.append(((lo, hi), copy))
    return out


def picked(sel_ref, src_ref, dst_ref, top_ref, start, count):
    tops = []
    for i in range(0, count, 2):
        width = min(2, count - i) * BLOCK
        at = pl.ds(start + i * BLOCK, width)
        got = jnp.dot(sel_ref[...], src_ref[:, at], preferred_element_type=F32)
        dst_ref[:, at] = got.astype(BF16)
        tops += [got[:, j : j + BLOCK] for j in range(0, width, BLOCK)]
    top_ref[...] = functools.reduce(jnp.maximum, tops, top_ref[...])


def send_kernel(
    rows, first, sb_dev,
    me_ref, mask_ref, dest_hbm, x_hbm, w_hbm, s_hbm, send_hbm, kept_hbm,
    x_buf, w_buf, s_buf, dest, sel, xc, kept, maps, stage, cols, facts,
    top, total, s_top, s_total, used,
    in_sem, x_sem, s_sem, kept_sem, out_sem, fact_sem,
):
    blocks = w_buf.shape[0]
    s_blocks = s_buf.shape[1] // BLOCK
    peers = send_hbm.shape[0]
    w_copy = pltpu.make_async_copy(w_hbm, w_buf, in_sem.at[0])
    w_copy.start()
    x_copies = column_copies(x_hbm, x_buf, x_sem, blocks, 3)
    ((_, s_copy),) = column_copies(s_hbm, s_buf, s_sem, s_blocks, 1)
    dest_copy = pltpu.make_async_copy(dest_hbm, dest, in_sem.at[1])
    dest_copy.start()
    sel[...] = selector(mask_ref[...].reshape(1, -1), rows, first)
    top[...] = jnp.full(top.shape, -jnp.inf, F32)
    s_top[...] = jnp.full(top.shape, -jnp.inf, F32)
    total[...] = jnp.zeros(total.shape, F32)
    s_total[...] = jnp.zeros(total.shape, F32)

    def clear(i, carry):
        used[i] = 0
        return carry

    lax.fori_loop(0, peers, clear, 0)
    w_copy.wait()
    ones = jnp.ones((K * BLOCK, BLOCK), BF16)

    def weight(b):
        both = jnp.concatenate([w_buf[b, k] for k in range(K)], axis=1)
        scale = 1.0 / jnp.dot(both, ones, preferred_element_type=F32)
        maps[b] = (both.astype(F32) * jnp.concatenate([scale] * K, axis=1)).astype(BF16)

    def teacher(i, count):
        start = i * GROUP * BLOCK
        if not isinstance(i, int):
            start = pl.multiple_of(start, GROUP * BLOCK)
        picked(sel, x_buf, xc, top, start, count)
        for j in range(count):
            weight(i * GROUP + j)

    def teachers(i, carry):
        teacher(i, GROUP)
        return carry

    for (lo, hi), copy in x_copies:
        copy.wait()
        lax.fori_loop(lo, hi, teachers, 0)
    if blocks % GROUP:
        teacher(blocks // GROUP, blocks % GROUP)
    highest = jnp.max(top[...], axis=1, keepdims=True)
    top[...] = jnp.broadcast_to(highest, top.shape)
    dest_copy.wait()
    s_copy.wait()
    base = me_ref[0] * blocks
    factor = (1 << 16) // sb_dev + 1
    assert all(d * factor >> 16 == d // sb_dev for d in range(peers * sb_dev))
    lane = iota((8, LANES), 1)

    def raised(b):
        at = pl.ds(pl.multiple_of(b * BLOCK, BLOCK), BLOCK)
        return jnp.exp(xc[:, at].astype(F32) - top[...])

    def tile(b, value, route):
        mapped = jnp.dot(value.astype(BF16), maps[b], preferred_element_type=F32)
        for k in range(K):
            stage[K * b + k] = mapped[:, k * BLOCK : (k + 1) * BLOCK].astype(BF16)
            block = dest[k, base + b]
            owner = lax.shift_right_logical(block * factor, 16)
            rank = used[owner]
            used[owner] = rank + 1
            near = (block - owner * sb_dev).astype(F32)
            route = jnp.where(lane == owner * CAP + rank, near, route)
            pltpu.make_async_copy(
                stage.at[K * b + k],
                send_hbm.at[owner, pl.ds(pl.multiple_of(rank * rows, 16), rows)],
                out_sem,
            ).start()
        return route

    def pair(i, route):
        one, two = raised(2 * i), raised(2 * i + 1)
        total[...] += one + two
        return tile(2 * i + 1, two, tile(2 * i, one, route))

    def both(i, route):
        picked(sel, s_buf, kept, s_top, pl.multiple_of(i * 2 * BLOCK, 2 * BLOCK), 2)
        return pair(i, route)

    shared = min(blocks, s_blocks) // 2
    route = lax.fori_loop(0, shared, both, jnp.full((8, LANES), sb_dev, F32))
    for i in range(shared, blocks // 2):
        route = pair(i, route)
    for b in range(2 * shared, s_blocks, 2):
        picked(sel, s_buf, kept, s_top, b * BLOCK, min(2, s_blocks - b))
    kept_copy = pltpu.make_async_copy(kept, kept_hbm, kept_sem)
    kept_copy.start()
    if blocks % 2:
        last = raised(blocks - 1)
        total[...] += last
        route = tile(blocks - 1, last, route)
    summed = jnp.sum(total[...], axis=1, keepdims=True)
    s_highest = jnp.max(s_top[...], axis=1, keepdims=True)
    s_top[...] = jnp.broadcast_to(s_highest, top.shape)

    def student(start, count):
        at = [pl.ds(start + i * BLOCK, BLOCK) for i in range(count)]
        s_total[...] += sum(jnp.exp(kept[:, a].astype(F32) - s_top[...]) for a in at)

    def students(i, carry):
        student(pl.multiple_of(i * GROUP * BLOCK, GROUP * BLOCK), GROUP)
        return carry

    lax.fori_loop(0, s_blocks // GROUP, students, 0)
    if s_blocks % GROUP:
        student(s_blocks // GROUP * GROUP * BLOCK, s_blocks % GROUP)
    s_summed = jnp.sum(s_total[...], axis=1, keepdims=True)
    columns = (highest, *parted(summed, 2), s_highest, *parted(s_summed, 2))
    full = rows // LANES
    rest = rows - full * LANES
    cols[...] = jnp.zeros(cols.shape, F32)
    cols[0:rows] = in_lanes(columns, rows)
    if rest:
        upper = [column[full * LANES :] for column in columns[VALUES // 2 :]]
        cols[full * LANES + LANES // 2 : full * LANES + LANES // 2 + rest] = in_lanes(upper, rest)
    total[0:FACTS] = jnp.zeros((FACTS, LANES), F32)
    for q in range(full + (rest > 0)):
        turned = cols[q * LANES : (q + 1) * LANES].T
        height = VALUES if q < full else VALUES // 2
        total[q * VALUES : q * VALUES + height] = turned[:height]
    total[ROUTE : ROUTE + 1] = route[0:1]
    facts[...] = jnp.broadcast_to(total[0:FACTS].astype(BF16)[None], facts.shape)
    fact_copy = pltpu.make_async_copy(
        facts, send_hbm.at[:, pl.ds(CAP * rows, FACTS)], fact_sem
    )
    fact_copy.start()
    pltpu.make_async_copy(stage, stage, out_sem).wait()
    kept_copy.wait()
    fact_copy.wait()


def combine_kernel(
    rows, first, chunk,
    me_ref, mask_ref, recv_hbm, s_ref, out_ref,
    buf, facts, facts32, share, near_vm, near, acc, cols, sems, fact_sem, near_sem,
):
    peers = recv_hbm.shape[0]
    blocks = s_ref.shape[1] // BLOCK
    spans = -(-rows // LANES)
    fact_copy = pltpu.make_async_copy(
        recv_hbm.at[:, pl.ds(CAP * rows, FACTS)], facts, fact_sem
    )
    fact_copy.start()

    def piece_copy(q, r):
        start = pl.multiple_of(q * chunk, chunk)
        return pltpu.make_async_copy(
            recv_hbm.at[:, pl.ds(r * rows + start, chunk)],
            buf.at[r, :, pl.ds(start, chunk)],
            sems.at[q, r],
        )

    for q in range(rows // chunk):
        for r in range(CAP):
            piece_copy(q, r).start()
    fact_copy.wait()
    facts32[...] = facts[...].astype(F32).reshape(facts32.shape)

    def fact(row):
        return facts32[pl.ds(row, peers, stride=FACTS), :]

    lane = iota((peers, LANES), 1)
    routes = fact(ROUTE)
    slots = jnp.zeros((peers, LANES), F32)
    for r in range(CAP):
        mine = jnp.where(lane == me_ref[0] * CAP + r, routes, 0.0)
        slots = jnp.where(lane == r, jnp.sum(mine, axis=1, keepdims=True), slots)
    near_vm[...] = slots.astype(jnp.int32)
    near_copy = pltpu.make_async_copy(near_vm, near, near_sem)
    near_copy.start()
    for q in range(spans):
        if (q + 1) * LANES <= rows:
            values = [fact(q * VALUES + v) for v in range(VALUES)]
        else:
            values = [fact(q * VALUES + v) for v in range(VALUES // 2)]
            values += [pltpu.roll(value, LANES // 2, 1) for value in values]
        highest, high, low, s_highest, s_high, s_low = values
        raised = jnp.exp(highest - jnp.max(highest, axis=0, keepdims=True))
        total = jnp.sum(raised * (high + low), axis=0, keepdims=True)
        part = raised * ((1.0 - SMOOTH) / total)
        s_top = jnp.max(s_highest, axis=0, keepdims=True)
        s_total = jnp.sum(jnp.exp(s_highest - s_top) * (s_high + s_low), axis=0, keepdims=True)
        norm = jnp.broadcast_to(s_top + jnp.log(s_total), (LANES - peers, LANES))
        share[q * LANES : (q + 1) * LANES] = jnp.concatenate([part, norm], axis=0).T
    cols[...] = jnp.zeros(cols.shape, F32)
    near_copy.wait()

    def work(q, carry):
        at = pl.ds(pl.multiple_of(q * chunk, chunk), chunk)
        shares = share[at]
        acc[...] = jnp.zeros(acc.shape, F32)
        for r in range(CAP):
            piece_copy(q, r).wait()
        for source in range(peers):
            scale = jnp.broadcast_to(shares[:, source : source + 1], (chunk, LANES))
            for r in range(CAP):
                acc[near[source, r]] += scale * buf[r, source, at].astype(F32)
        norm = jnp.broadcast_to(shares[:, peers : peers + 1], (chunk, LANES))

        def block(j, cross):
            target = acc[j] + SMOOTH / VS
            student = s_ref[at, pl.ds(pl.multiple_of(j * BLOCK, BLOCK), BLOCK)].astype(F32)
            return cross + target * (jnp.log(target) - (student - norm))

        cross = lax.fori_loop(0, blocks, block, jnp.zeros((chunk, LANES), F32))
        cols[at] = jnp.broadcast_to(jnp.sum(cross, axis=1, keepdims=True), (chunk, LANES))
        return carry

    lax.fori_loop(0, rows // chunk, work, 0)
    counted = jnp.sum(mask_ref[...].reshape(1, -1).astype(F32), axis=1, keepdims=True)
    row = iota((8, LANES), 0)
    place = iota((8, LANES), 1)
    values = jnp.zeros((8, LANES), F32)
    part = jnp.zeros((8, LANES), F32)
    for q in range(spans):
        kl = cols[q * LANES : (q + 1) * LANES].T[:8]
        ahead = place + q * LANES
        kl = jnp.where((ahead < rows) & ((ahead + first).astype(F32) < counted), kl, 0.0)
        values = jnp.where(row % 4 == q, kl, values)
        part = part + kl
    whole_sum = jnp.broadcast_to(jnp.sum(part, axis=1, keepdims=True), (8, LANES))
    tally = jnp.where(place == 0, whole_sum, jnp.where(place == 1, counted, 0.0))
    values = jnp.where(row % 4 == 3, tally, values)
    for d in range(peers // 2):
        out_ref[d * 8 : (d + 1) * 8] = values


def tally_kernel(all_ref, out_ref):
    peers = all_ref.shape[0] // 4
    sums = jnp.sum(all_ref[pl.ds(3, peers, stride=4), :], axis=0, keepdims=True)
    lane = iota((1, LANES), 1)
    sums = jnp.where(lane == 1, sums * (1.0 / peers), sums)
    out_ref[...] = jnp.broadcast_to(sums, out_ref.shape)


def loss_kernel(rows, first, all_ref, mask_ref, loss_ref):
    peers = all_ref.shape[0] // 4
    spans = -(-rows // LANES)
    kl = jnp.concatenate(
        [
            jnp.sum(all_ref[pl.ds(q, peers, stride=4), :], axis=0, keepdims=True)
            for q in range(spans)
        ],
        axis=1,
    )
    mask = mask_ref[...].reshape(1, -1)
    width = spans * LANES
    row = iota((16, width), 0)
    parts = jnp.zeros((16, width), F32)
    for v, part in enumerate(parted(kl, 3)):
        parts = jnp.where(row == v, jnp.broadcast_to(part, (16, width)), parts)
    back = jnp.dot(parts.astype(BF16), selector(mask, width, first), preferred_element_type=F32)
    loss = jnp.sum(back, axis=0, keepdims=True) * mask.astype(F32)
    loss_ref[...] = loss.reshape(loss_ref.shape)


def close_kernel(rows, tally_ref, mean_ref, over_ref):
    lane = iota((1, LANES), 1)
    sums = jnp.sum(tally_ref[...], axis=0, keepdims=True)
    most = jnp.max(tally_ref[...], axis=0, keepdims=True)
    total = jnp.sum(jnp.where(lane == 0, sums, 0.0), axis=1, keepdims=True)
    count = jnp.sum(jnp.where(lane == 1, sums, 0.0), axis=1, keepdims=True)
    mean_ref[0] = jnp.sum(total / count)
    over_ref[0] = jnp.max(jnp.where((lane == 1) & (most > rows), 1, 0))


def whole(memory_space):
    return pl.BlockSpec(memory_space=memory_space)


VM, SM, HB = pltpu.VMEM, pltpu.SMEM, pltpu.HBM
SMALL = pltpu.CompilerParams(vmem_limit_bytes=6 << 20)


def exchanged(teacher_logits, student_logits, dest, tile_weight, mask, rows, first):
    peers = lax.axis_size("vocab")
    groups = lax.axis_size("dp")
    me = lax.axis_index("vocab").astype(jnp.int32).reshape(1)
    tokens = teacher_logits.shape[0]
    tb_dev = teacher_logits.shape[1] // BLOCK
    sb_dev = student_logits.shape[1] // BLOCK
    wide = -(-rows // LANES) * LANES
    tiles = tb_dev * K
    dma = pltpu.SemaphoreType.DMA
    tall = max(rows, LANES)
    send, kept = pl.pallas_call(
        functools.partial(send_kernel, rows, first, sb_dev),
        out_shape=(
            jax.ShapeDtypeStruct((peers, CAP * rows + FACTS, LANES), BF16),
            jax.ShapeDtypeStruct((rows, student_logits.shape[1]), BF16),
        ),
        in_specs=[whole(SM), whole(VM), whole(HB), whole(HB), whole(HB), whole(HB)],
        out_specs=(whole(HB), whole(HB)),
        scratch_shapes=[
            VM(teacher_logits.shape, BF16),
            VM(tile_weight.shape, BF16),
            VM(student_logits.shape, BF16),
            SM(dest.shape, jnp.int32),
            VM((rows, tokens), BF16),
            VM((rows, tb_dev * BLOCK), BF16),
            VM((rows, sb_dev * BLOCK), BF16),
            VM((tb_dev, BLOCK, K * BLOCK), BF16),
            VM((tiles, rows, BLOCK), BF16),
            VM((wide, LANES), F32),
            VM((peers, FACTS, LANES), BF16),
            VM((rows, LANES), F32),
            VM((rows, LANES), F32),
            VM((rows, LANES), F32),
            VM((rows, LANES), F32),
            SM((peers,), jnp.int32),
            dma((2,)),
            dma((3,)),
            dma((1,)),
            dma(()),
            dma(()),
            dma(()),
        ],
        compiler_params=pltpu.CompilerParams(vmem_limit_bytes=56 << 20),
        name="send",
    )(me, mask, dest, teacher_logits, tile_weight, student_logits)
    received = lax.all_to_all(send, "vocab", 0, 0, tiled=True)
    chunk = rows // 4 if rows % 64 == 0 else rows
    mine = pl.pallas_call(
        functools.partial(combine_kernel, rows, first, chunk),
        out_shape=jax.ShapeDtypeStruct((peers * 4, LANES), F32),
        in_specs=[whole(SM), whole(VM), whole(HB), whole(VM)],
        out_specs=whole(VM),
        scratch_shapes=[
            VM((CAP, peers, rows, LANES), BF16),
            VM((peers, FACTS, LANES), BF16),
            VM((peers * FACTS, LANES), F32),
            VM((wide, LANES), F32),
            VM((peers, LANES), jnp.int32),
            SM((peers, LANES), jnp.int32),
            VM((sb_dev + 1, chunk, LANES), F32),
            VM((wide, LANES), F32),
            dma((rows // chunk, CAP)),
            dma(()),
            dma(()),
        ],
        compiler_params=pltpu.CompilerParams(vmem_limit_bytes=40 << 20),
        name="combine",
    )(me, mask, received, kept)
    collected = lax.all_to_all(mine, "vocab", 0, 0, tiled=True)
    tally = pl.pallas_call(
        tally_kernel,
        out_shape=jax.ShapeDtypeStruct((groups, LANES), F32),
        in_specs=[whole(VM)],
        out_specs=whole(VM),
        compiler_params=SMALL,
        name="tally",
    )(collected)
    tally = lax.all_to_all(tally, "dp", 0, 0, tiled=True)
    loss = pl.pallas_call(
        functools.partial(loss_kernel, rows, first),
        out_shape=jax.ShapeDtypeStruct((tokens,), F32),
        in_specs=[whole(VM), whole(VM)],
        out_specs=whole(VM),
        cost_estimate=pl.CostEstimate(flops=10**10, bytes_accessed=10**6, transcendentals=0),
        compiler_params=SMALL,
        name="loss",
    )(collected, mask)
    mean, over = pl.pallas_call(
        functools.partial(close_kernel, rows),
        out_shape=(jax.ShapeDtypeStruct((1,), F32), jax.ShapeDtypeStruct((1,), jnp.int32)),
        in_specs=[whole(VM)],
        out_specs=(whole(SM), whole(SM)),
        compiler_params=SMALL,
        name="close",
    )(tally)
    return loss, mean.reshape(()), over.reshape(())


def local(teacher_logits, student_logits, tile_dest, tile_weight, token_mask):
    tokens = teacher_logits.shape[0]
    parts = (teacher_logits, student_logits, tile_dest.T, tile_weight, token_mask)
    rows = tokens * 5 // 6 if tokens % 384 == 0 else tokens
    loss, mean, over = exchanged(*parts, rows, 0)
    if rows < tokens:

        def rest():
            more, more_mean, _ = exchanged(*parts, tokens - rows, rows)
            return loss + more, mean + more_mean

        loss, mean = lax.cond(over > 0, rest, lambda: (loss, mean))
    return loss, mean


def solution(mesh):
    in_specs = (P("dp", "vocab"), P("dp", "vocab"), P(), P("vocab", None, None, None), P("dp"))
    out_specs = (P("dp"), P())
    return jax.shard_map(local, mesh=mesh, in_specs=in_specs, out_specs=out_specs, check_vma=False)
```

time: 171 us -> 153 us (0.89)
  waiting for transfers between devices: 19 us -> 6.17 us
  blocking collectives: 102 us -> 112 us
  Pallas kernels: 30.8 us -> 23.8 us
  starting transfers between devices: 13.1 us -> 8.19 us
  between operations: 3.74 us -> 1.38 us
    all_to_all x1, waiting for transfers between devices: 19 us -> 6.17 us  [exchanged(): tally = lax.all_to_all(tally, 'dp', 0, 0, tiled=True)]
    all_to_all x0 -> x1, blocking collectives: none -> 12.1 us  [exchanged(): collected = lax.all_to_all(mine, 'vocab', 0, 0, tiled=True)]
    pallas_call x1, Pallas kernels: 20.1 us -> 14.4 us  [exchanged(): pl.pallas_call(functools.partial(send_kernel, rows, first, sb_dev), out_s...]
    all_to_all x1, starting transfers between devices: 13.1 us -> 8.19 us  [exchanged(): tally = lax.all_to_all(tally, 'dp', 0, 0, tiled=True)]
    pallas_call x2 -> x4, Pallas kernels: 10.7 us -> 9.42 us  [the longest x1 7.77 us: exchanged(): pl.pallas_call(functools.partial(combine_kernel, rows, first, chunk), out...]
where the time goes in v3:
time: 153 us
  blocking collectives  112 us (73%)
  Pallas kernels  23.8 us (16%)
  starting transfers between devices  8.19 us (5%)
  waiting for transfers between devices  6.17 us (4%)
    all_to_all x1, blocking collectives, exchanged(): received = lax.all_to_all(send, 'vocab', 0, 0, tiled=True)  100 us
    pallas_call x1, Pallas kernels, exchanged(): pl.pallas_call(functools.partial(send_kernel, rows, first, sb_dev), out_s...  14.4 us
    all_to_all x1, blocking collectives, exchanged(): collected = lax.all_to_all(mine, 'vocab', 0, 0, tiled=True)  12.1 us
    all_to_all x1, starting transfers between devices, exchanged(): tally = lax.all_to_all(tally, 'dp', 0, 0, tiled=True)  8.19 us
    pallas_call x1, Pallas kernels, exchanged(): pl.pallas_call(functools.partial(combine_kernel, rows, first, chunk), out...  7.77 us
    all_to_all x1, waiting for transfers between devices, exchanged(): tally = lax.all_to_all(tally, 'dp', 0, 0, tiled=True)  6.17 us
  transfers between devices with their start and end apart: 1, of which 1 were waited for; matrix products, arithmetic and copies ran while one was open for 0% of the time, Pallas kernels for 0%

profile of v3, /device:TPU:1, one launch (start us, length us, event | category | flops | bytes accessed | tf_op | source)
XLA Modules:
  0.0 152.5 jit_solution(16814887197840619062)
XLA Ops:
  0.6 14.4 %send.3 = (bf16[32,976,128]{2,1,0:T(8,128)(2,1)}, bf16[320,3968]{1,0:T(8,128)(2,1)}) custom-call(s32[1]{0:T(128)} %bitcast.8.me_ref, s32[384]{0:T(512)} %mask_ref.5, s32[2,1184]{1,0:T(2,128)} %bitcast.26, bf16[384,4736]{1,0:T(8,128)(2,1)} %x_hbm.1, bf16[37,2,128,128]{3,2,1,0:T(8,128)(2,1)} %w_hbm.1, bf16[384,3968]{1,0:T(8,128)(2,1)} %s_hbm.1), custom_call_target="tpu_custom_call" | custom-call | tf_op jit(solution)/shard_map/send/pallas_call | solution.py:377
  15.0 0.0 copy-start
  15.0 0.0 copy-start.4
  15.1 100.3 %all_to_all.49.recv_hbm = bf16[32,976,128]{2,1,0:T(8,128)(2,1)S(1)} all-to-all(bf16[32,976,128]{2,1,0:T(8,128)(2,1)} %get-tuple-element.34), channel_id=1, replica_groups=mesh['dp'=8,'vocab'=32] {'vocab'}, dimensions={0} | all-to-all | bytes 15990784 | tf_op jit(solution)/shard_map/all_to_all | solution.py:412
  115.3 0.0 copy-done
  115.3 0.0 copy-done.4
  115.3 7.8 %combine.3 = f32[128,128]{1,0:T(8,128)S(1)} custom-call(s32[1]{0:T(128)} %bitcast.8.me_ref, s32[384]{0:T(512)S(1)} %copy-done.4, bf16[32,976,128]{2,1,0:T(8,128)(2,1)S(1)} %all_to_all.49.recv_hbm, bf16[320,3968]{1,0:T(8,128)(2,1)S(1)} %copy-done), custom_call_target="tpu_custom_call" | custom-call | tf_op jit(solution)/shard_map/combine/pallas_call | solution.py:414
  123.1 12.1 %all_to_all.50 = f32[32,4,128]{2,1,0:T(4,128)S(1)} all-to-all(f32[32,4,128]{2,1,0:T(4,128)S(1)} %bitcast.18), channel_id=1, replica_groups=mesh['dp'=8,'vocab'=32] {'vocab'}, dimensions={0} | all-to-all | bytes 131072 | tf_op jit(solution)/shard_map/all_to_all | solution.py:435
  135.2 0.6 tally.3
  135.8 8.2 %all-to-all-start.5 = ((f32[8,1,128]{2,1,0:T(1,128)}), f32[8,1,128]{2,1,0:T(1,128)S(1)}, u32[]{:S(2)}, u32[]{:S(2)}) async-start(f32[8,1,128]{2,1,0:T(1,128)} %bitcast.13), calls=%async_computation.5 | async-start | bytes 8192 | tf_op jit(solution)/shard_map/all_to_all | solution.py:444
  144.0 0.0 copy-start.2
  144.0 0.0 copy-start.3
  144.0 0.3 loss.3
  144.4 6.2 %all-to-all-done.5 = f32[8,1,128]{2,1,0:T(1,128)S(1)} async-done(((f32[8,1,128]{2,1,0:T(1,128)}), f32[8,1,128]{2,1,0:T(1,128)S(1)}, u32[]{:S(2)}, u32[]{:S(2)}) %all-to-all-start.5) | async-done | bytes 4128 | tf_op jit(solution)/shard_map/all_to_all | solution.py:444
  150.5 0.7 close.3
  151.9 0.0 copy-done.2
  151.9 0.0 copy-done.3
  152.0 0.0 copy-start.5
  152.0 0.6 copy-done.5
  (1 shorter events, 0.0 us)
Async XLA Ops:
  15.0 100.3 %copy-start = (bf16[320,3968]{1,0:T(8,128)(2,1)S(1)}, bf16[320,3968]{1,0:T(8,128)(2,1)}, u32[]{:S(2)}) copy-start(bf16[320,3968]{1,0:T(8,128)(2,1)} %get-tuple-element.35.s_ref) | copy-start | bytes 7618564
  15.0 100.3 %copy-start.4 = (s32[384]{0:T(512)S(1)}, s32[384]{0:T(512)}, u32[]{:S(2)}) copy-start(s32[384]{0:T(512)} %mask_ref.5) | copy-start | bytes 4612
  135.8 14.7 %all-to-all-start.5 = ((f32[8,1,128]{2,1,0:T(1,128)}), f32[8,1,128]{2,1,0:T(1,128)S(1)}, u32[]{:S(2)}, u32[]{:S(2)}) async-start(f32[8,1,128]{2,1,0:T(1,128)} %bitcast.13), calls=%async_computation.5 | async-start | bytes 8192 | tf_op jit(solution)/shard_map/all_to_all | solution.py:444
  144.0 7.9 %copy-start.2 = (bf16[384,3968]{1,0:T(8,128)(2,1)S(1)}, bf16[384,3968]{1,0:T(8,128)(2,1)}, u32[]{:S(2)}) copy-start(bf16[384,3968]{1,0:T(8,128)(2,1)} %s_hbm.1) | copy-start | bytes 9142276
  144.0 7.9 %copy-start.3 = (s32[1184,2]{0,1:T(2,128)S(1)}, s32[1184,2]{0,1:T(2,128)}, u32[]{:S(2)}) copy-start(s32[1184,2]{0,1:T(2,128)} %param.9) | copy-start | bytes 28420
  152.0 0.6 copy-start.5

commit v4 on v3

--- a/solution.py
+++ b/solution.py
@@ -13,7 +13,7 @@
 CAP = 3
 SMOOTH = 0.1
 LANES = 128
-GROUP = 4
+GROUP = 8
 FACTS = 16
 ROUTE = 15
 VALUES = 6
@@ -79,14 +79,14 @@
 
 def send_kernel(
     rows, first, sb_dev,
-    me_ref, mask_ref, dest_hbm, x_hbm, w_hbm, s_hbm, send_hbm, kept_hbm,
-    x_buf, w_buf, s_buf, dest, sel, xc, kept, maps, stage, cols, facts,
+    me_ref, mask_ref, dest_hbm, x_hbm, w_hbm, s_hbm, send_ref, kept,
+    x_buf, w_buf, s_buf, dest, sel, xc, maps, cols,
     top, total, s_top, s_total, used,
-    in_sem, x_sem, s_sem, kept_sem, out_sem, fact_sem,
+    in_sem, x_sem, s_sem,
 ):
     blocks = w_buf.shape[0]
     s_blocks = s_buf.shape[1] // BLOCK
-    peers = send_hbm.shape[0]
+    peers = send_ref.shape[0]
     w_copy = pltpu.make_async_copy(w_hbm, w_buf, in_sem.at[0])
     w_copy.start()
     x_copies = column_copies(x_hbm, x_buf, x_sem, blocks, 3)
@@ -145,18 +145,14 @@
     def tile(b, value, route):
         mapped = jnp.dot(value.astype(BF16), maps[b], preferred_element_type=F32)
         for k in range(K):
-            stage[K * b + k] = mapped[:, k * BLOCK : (k + 1) * BLOCK].astype(BF16)
             block = dest[k, base + b]
             owner = lax.shift_right_logical(block * factor, 16)
             rank = used[owner]
             used[owner] = rank + 1
             near = (block - owner * sb_dev).astype(F32)
             route = jnp.where(lane == owner * CAP + rank, near, route)
-            pltpu.make_async_copy(
-                stage.at[K * b + k],
-                send_hbm.at[owner, pl.ds(pl.multiple_of(rank * rows, 16), rows)],
-                out_sem,
-            ).start()
+            at = pl.ds(pl.multiple_of(rank * rows, 16), rows)
+            send_ref[owner, at] = mapped[:, k * BLOCK : (k + 1) * BLOCK].astype(BF16)
         return route
 
     def pair(i, route):
@@ -165,17 +161,15 @@
         return tile(2 * i + 1, two, tile(2 * i, one, route))
 
     def both(i, route):
-        picked(sel, s_buf, kept, s_top, pl.multiple_of(i * 2 * BLOCK, 2 * BLOCK), 2)
-        return pair(i, route)
-
-    shared = min(blocks, s_blocks) // 2
-    route = lax.fori_loop(0, shared, both, jnp.full((8, LANES), sb_dev, F32))
+        picked(sel, s_buf, kept, s_top, pl.multiple_of(i * 4 * BLOCK, 4 * BLOCK), 4)
+        return pair(2 * i + 1, pair(2 * i, route))
+
+    shared = min(blocks, s_blocks) // 4 * 2
+    route = lax.fori_loop(0, shared // 2, both, jnp.full((8, LANES), sb_dev, F32))
     for i in range(shared, blocks // 2):
         route = pair(i, route)
     for b in range(2 * shared, s_blocks, 2):
         picked(sel, s_buf, kept, s_top, b * BLOCK, min(2, s_blocks - b))
-    kept_copy = pltpu.make_async_copy(kept, kept_hbm, kept_sem)
-    kept_copy.start()
     if blocks % 2:
         last = raised(blocks - 1)
         total[...] += last
@@ -210,42 +204,21 @@
         height = VALUES if q < full else VALUES // 2
         total[q * VALUES : q * VALUES + height] = turned[:height]
     total[ROUTE : ROUTE + 1] = route[0:1]
-    facts[...] = jnp.broadcast_to(total[0:FACTS].astype(BF16)[None], facts.shape)
-    fact_copy = pltpu.make_async_copy(
-        facts, send_hbm.at[:, pl.ds(CAP * rows, FACTS)], fact_sem
-    )
-    fact_copy.start()
-    pltpu.make_async_copy(stage, stage, out_sem).wait()
-    kept_copy.wait()
-    fact_copy.wait()
+    facts = total[0:FACTS].astype(BF16)
+    for d in range(peers):
+        send_ref[d, CAP * rows : CAP * rows + FACTS] = facts
 
 
 def combine_kernel(
     rows, first, chunk,
-    me_ref, mask_ref, recv_hbm, s_ref, out_ref,
-    buf, facts, facts32, share, near_vm, near, acc, cols, sems, fact_sem, near_sem,
+    me_ref, mask_ref, recv_ref, s_ref, out_ref,
+    facts32, share, near_vm, near, acc, cols, near_sem,
 ):
-    peers = recv_hbm.shape[0]
+    peers = recv_ref.shape[0]
     blocks = s_ref.shape[1] // BLOCK
     spans = -(-rows // LANES)
-    fact_copy = pltpu.make_async_copy(
-        recv_hbm.at[:, pl.ds(CAP * rows, FACTS)], facts, fact_sem
-    )
-    fact_copy.start()
-
-    def piece_copy(q, r):
-        start = pl.multiple_of(q * chunk, chunk)
-        return pltpu.make_async_copy(
-            recv_hbm.at[:, pl.ds(r * rows + start, chunk)],
-            buf.at[r, :, pl.ds(start, chunk)],
-            sems.at[q, r],
-        )
-
-    for q in range(rows // chunk):
-        for r in range(CAP):
-            piece_copy(q, r).start()
-    fact_copy.wait()
-    facts32[...] = facts[...].astype(F32).reshape(facts32.shape)
+    facts = recv_ref[:, CAP * rows : CAP * rows + FACTS]
+    facts32[...] = facts.astype(F32).reshape(facts32.shape)
 
     def fact(row):
         return facts32[pl.ds(row, peers, stride=FACTS), :]
@@ -280,12 +253,11 @@
         at = pl.ds(pl.multiple_of(q * chunk, chunk), chunk)
         shares = share[at]
         acc[...] = jnp.zeros(acc.shape, F32)
-        for r in range(CAP):
-            piece_copy(q, r).wait()
         for source in range(peers):
             scale = jnp.broadcast_to(shares[:, source : source + 1], (chunk, LANES))
             for r in range(CAP):
-                acc[near[source, r]] += scale * buf[r, source, at].astype(F32)
+                piece = recv_ref[source, pl.ds(pl.multiple_of(r * rows + q * chunk, 16), chunk)]
+                acc[near[source, r]] += scale * piece.astype(F32)
         norm = jnp.broadcast_to(shares[:, peers : peers + 1], (chunk, LANES))
 
         def block(j, cross):
@@ -371,7 +343,6 @@
     tb_dev = teacher_logits.shape[1] // BLOCK
     sb_dev = student_logits.shape[1] // BLOCK
     wide = -(-rows // LANES) * LANES
-    tiles = tb_dev * K
     dma = pltpu.SemaphoreType.DMA
     tall = max(rows, LANES)
     send, kept = pl.pallas_call(
@@ -381,7 +352,7 @@
             jax.ShapeDtypeStruct((rows, student_logits.shape[1]), BF16),
         ),
         in_specs=[whole(SM), whole(VM), whole(HB), whole(HB), whole(HB), whole(HB)],
-        out_specs=(whole(HB), whole(HB)),
+        out_specs=(whole(VM), whole(VM)),
         scratch_shapes=[
             VM(teacher_logits.shape, BF16),
             VM(tile_weight.shape, BF16),
@@ -389,11 +360,8 @@
             SM(dest.shape, jnp.int32),
             VM((rows, tokens), BF16),
             VM((rows, tb_dev * BLOCK), BF16),
-            VM((rows, sb_dev * BLOCK), BF16),
             VM((tb_dev, BLOCK, K * BLOCK), BF16),
-            VM((tiles, rows, BLOCK), BF16),
             VM((wide, LANES), F32),
-            VM((peers, FACTS, LANES), BF16),
             VM((rows, LANES), F32),
             VM((rows, LANES), F32),
             VM((rows, LANES), F32),
@@ -402,34 +370,27 @@
             dma((2,)),
             dma((3,)),
             dma((1,)),
-            dma(()),
-            dma(()),
-            dma(()),
         ],
-        compiler_params=pltpu.CompilerParams(vmem_limit_bytes=56 << 20),
+        compiler_params=pltpu.CompilerParams(vmem_limit_bytes=34 << 20),
         name="send",
     )(me, mask, dest, teacher_logits, tile_weight, student_logits)
     received = lax.all_to_all(send, "vocab", 0, 0, tiled=True)
-    chunk = rows // 4 if rows % 64 == 0 else rows
+    chunk = rows // 2 if rows % 64 == 0 else rows
     mine = pl.pallas_call(
         functools.partial(combine_kernel, rows, first, chunk),
         out_shape=jax.ShapeDtypeStruct((peers * 4, LANES), F32),
-        in_specs=[whole(SM), whole(VM), whole(HB), whole(VM)],
+        in_specs=[whole(SM), whole(VM), whole(VM), whole(VM)],
         out_specs=whole(VM),
         scratch_shapes=[
-            VM((CAP, peers, rows, LANES), BF16),
-            VM((peers, FACTS, LANES), BF16),
             VM((peers * FACTS, LANES), F32),
             VM((wide, LANES), F32),
             VM((peers, LANES), jnp.int32),
             SM((peers, LANES), jnp.int32),
             VM((sb_dev + 1, chunk, LANES), F32),
             VM((wide, LANES), F32),
-            dma((rows // chunk, CAP)),
-            dma(()),
             dma(()),
         ],
-        compiler_params=pltpu.CompilerParams(vmem_limit_bytes=40 << 20),
+        compiler_params=pltpu.CompilerParams(vmem_limit_bytes=20 << 20),
         name="combine",
     )(me, mask, received, kept)
     collected = lax.all_to_all(mine, "vocab", 0, 0, tiled=True)

time: 153 us -> 148 us (0.967)
  Pallas kernels: 23.8 us -> 18.9 us
    pallas_call x1, Pallas kernels: 14.4 us -> 11.5 us  [exchanged(): pl.pallas_call(functools.partial(send_kernel, rows, first, sb_dev), out_s...]
    pallas_call x1, Pallas kernels: 7.77 us -> 5.78 us  [exchanged(): pl.pallas_call(functools.partial(combine_kernel, rows, first, chunk), out...]
where the time goes in v4:
time: 148 us; the launch traced here: 147 us
  blocking collectives  112 us (76%)
  Pallas kernels  18.9 us (13%)
  starting transfers between devices  8.18 us (6%)
  waiting for transfers between devices  6.18 us (4%)
    all_to_all x1, blocking collectives, exchanged(): received = lax.all_to_all(send, 'vocab', 0, 0, tiled=True)  99.9 us
    all_to_all x1, blocking collectives, exchanged(): collected = lax.all_to_all(mine, 'vocab', 0, 0, tiled=True)  12.1 us
    pallas_call x1, Pallas kernels, exchanged(): pl.pallas_call(functools.partial(send_kernel, rows, first, sb_dev), out_s...  11.5 us
    all_to_all x1, starting transfers between devices, exchanged(): tally = lax.all_to_all(tally, 'dp', 0, 0, tiled=True)  8.18 us
    all_to_all x1, waiting for transfers between devices, exchanged(): tally = lax.all_to_all(tally, 'dp', 0, 0, tiled=True)  6.18 us
    pallas_call x1, Pallas kernels, exchanged(): pl.pallas_call(functools.partial(combine_kernel, rows, first, chunk), out...  5.78 us
  transfers between devices with their start and end apart: 1, of which 1 were waited for; matrix products, arithmetic and copies ran while one was open for 0% of the time, Pallas kernels for 0%

profile of v4, /device:TPU:1, one launch (start us, length us, event | category | flops | bytes accessed | tf_op | source)
XLA Modules:
  0.0 147.3 jit_solution(7454892309253064351)
XLA Ops:
  0.6 11.5 %send.3 = (bf16[32,976,128]{2,1,0:T(8,128)(2,1)S(1)}, bf16[320,3968]{1,0:T(8,128)(2,1)S(1)}) custom-call(s32[1]{0:T(128)} %bitcast.8.me_ref, s32[384]{0:T(512)} %mask_ref.5, s32[2,1184]{1,0:T(2,128)} %bitcast.26, bf16[384,4736]{1,0:T(8,128)(2,1)} %x_hbm.1, bf16[37,2,128,128]{3,2,1,0:T(8,128)(2,1)} %w_hbm.1, bf16[384,3968]{1,0:T(8,128)(2,1)} %s_hbm.1), custom_call_target="tpu_custom_call" | custom-call | tf_op jit(solution)/shard_map/send/pallas_call | solution.py:348
  12.2 0.0 copy-start.2
  12.2 99.9 %all_to_all.49.recv_ref = bf16[32,976,128]{2,1,0:T(8,128)(2,1)S(1)} all-to-all(bf16[32,976,128]{2,1,0:T(8,128)(2,1)S(1)} %get-tuple-element.34), channel_id=1, replica_groups=mesh['dp'=8,'vocab'=32] {'vocab'}, dimensions={0} | all-to-all | bytes 15990784 | tf_op jit(solution)/shard_map/all_to_all | solution.py:377
  112.1 0.0 copy-done.2
  112.1 5.8 %combine.3 = f32[128,128]{1,0:T(8,128)S(1)} custom-call(s32[1]{0:T(128)} %bitcast.8.me_ref, s32[384]{0:T(512)S(1)} %copy-done.2, bf16[32,976,128]{2,1,0:T(8,128)(2,1)S(1)} %all_to_all.49.recv_ref, bf16[320,3968]{1,0:T(8,128)(2,1)S(1)} %get-tuple-element.35.s_ref), custom_call_target="tpu_custom_call" | custom-call | tf_op jit(solution)/shard_map/combine/pallas_call | solution.py:379
  117.9 12.1 %all_to_all.50 = f32[32,4,128]{2,1,0:T(4,128)S(1)} all-to-all(f32[32,4,128]{2,1,0:T(4,128)S(1)} %bitcast.18), channel_id=1, replica_groups=mesh['dp'=8,'vocab'=32] {'vocab'}, dimensions={0} | all-to-all | bytes 131072 | tf_op jit(solution)/shard_map/all_to_all | solution.py:396
  129.9 0.6 tally.3
  130.6 8.2 %all-to-all-start.5 = ((f32[8,1,128]{2,1,0:T(1,128)}), f32[8,1,128]{2,1,0:T(1,128)S(1)}, u32[]{:S(2)}, u32[]{:S(2)}) async-start(f32[8,1,128]{2,1,0:T(1,128)} %bitcast.13), calls=%async_computation.5 | async-start | bytes 8192 | tf_op jit(solution)/shard_map/all_to_all | solution.py:405
  138.7 0.0 copy-start
  138.7 0.0 copy-start.1
  138.8 0.3 loss.3
  139.1 6.2 %all-to-all-done.5 = f32[8,1,128]{2,1,0:T(1,128)S(1)} async-done(((f32[8,1,128]{2,1,0:T(1,128)}), f32[8,1,128]{2,1,0:T(1,128)S(1)}, u32[]{:S(2)}, u32[]{:S(2)}) %all-to-all-start.5) | async-done | bytes 4128 | tf_op jit(solution)/shard_map/all_to_all | solution.py:405
  145.3 0.7 close.3
  146.7 0.0 copy-done
  146.7 0.0 copy-done.1
  146.7 0.0 copy-start.3
  146.7 0.6 copy-done.3
  (1 shorter events, 0.0 us)
Async XLA Ops:
  12.2 100.0 %copy-start.2 = (s32[384]{0:T(512)S(1)}, s32[384]{0:T(512)}, u32[]{:S(2)}) copy-start(s32[384]{0:T(512)} %mask_ref.5) | copy-start | bytes 4612
  130.6 14.7 %all-to-all-start.5 = ((f32[8,1,128]{2,1,0:T(1,128)}), f32[8,1,128]{2,1,0:T(1,128)S(1)}, u32[]{:S(2)}, u32[]{:S(2)}) async-start(f32[8,1,128]{2,1,0:T(1,128)} %bitcast.13), calls=%async_computation.5 | async-start | bytes 8192 | tf_op jit(solution)/shard_map/all_to_all | solution.py:405
  138.7 7.9 %copy-start = (bf16[384,3968]{1,0:T(8,128)(2,1)S(1)}, bf16[384,3968]{1,0:T(8,128)(2,1)}, u32[]{:S(2)}) copy-start(bf16[384,3968]{1,0:T(8,128)(2,1)} %s_hbm.1) | copy-start | bytes 9142276
  138.7 7.9 %copy-start.1 = (s32[1184,2]{0,1:T(2,128)S(1)}, s32[1184,2]{0,1:T(2,128)}, u32[]{:S(2)}) copy-start(s32[1184,2]{0,1:T(2,128)} %param.9) | copy-start | bytes 28420
  146.7 0.6 copy-start.3

commit v5 on v4

--- a/solution.py
+++ b/solution.py
@@ -14,11 +14,15 @@
 SMOOTH = 0.1
 LANES = 128
 GROUP = 8
-FACTS = 16
-ROUTE = 15
 VALUES = 6
 F32 = jnp.float32
 BF16 = jnp.bfloat16
+
+
+def fact_rows(rows):
+    full, rest = divmod(rows, LANES)
+    needed = VALUES * full + (rest > 0) * VALUES // (1 + (rest <= LANES // 2)) + 1
+    return -(-needed // 16) * 16
 
 
 def iota(shape, dim):
@@ -75,6 +79,11 @@
         dst_ref[:, at] = got.astype(BF16)
         tops += [got[:, j : j + BLOCK] for j in range(0, width, BLOCK)]
     top_ref[...] = functools.reduce(jnp.maximum, tops, top_ref[...])
+
+
+def size_kernel(sizes, mask_ref, which_ref):
+    kept = jnp.sum(mask_ref[...].reshape(1, -1).astype(F32))
+    which_ref[0] = sum((kept > size).astype(jnp.int32) for size in sizes[:-1]) + 0
 
 
 def send_kernel(
@@ -191,40 +200,42 @@
         student(s_blocks // GROUP * GROUP * BLOCK, s_blocks % GROUP)
     s_summed = jnp.sum(s_total[...], axis=1, keepdims=True)
     columns = (highest, *parted(summed, 2), s_highest, *parted(s_summed, 2))
-    full = rows // LANES
-    rest = rows - full * LANES
+    full, rest = divmod(rows, LANES)
+    half = 0 < rest <= LANES // 2
+    facts = fact_rows(rows)
     cols[...] = jnp.zeros(cols.shape, F32)
     cols[0:rows] = in_lanes(columns, rows)
-    if rest:
+    if half:
         upper = [column[full * LANES :] for column in columns[VALUES // 2 :]]
         cols[full * LANES + LANES // 2 : full * LANES + LANES // 2 + rest] = in_lanes(upper, rest)
-    total[0:FACTS] = jnp.zeros((FACTS, LANES), F32)
+    total[0:facts] = jnp.zeros((facts, LANES), F32)
     for q in range(full + (rest > 0)):
         turned = cols[q * LANES : (q + 1) * LANES].T
-        height = VALUES if q < full else VALUES // 2
+        height = VALUES // 2 if half and q == full else VALUES
         total[q * VALUES : q * VALUES + height] = turned[:height]
-    total[ROUTE : ROUTE + 1] = route[0:1]
-    facts = total[0:FACTS].astype(BF16)
+    total[facts - 1 : facts] = route[0:1]
+    packed = total[0:facts].astype(BF16)
     for d in range(peers):
-        send_ref[d, CAP * rows : CAP * rows + FACTS] = facts
+        send_ref[d, CAP * rows : CAP * rows + facts] = packed
 
 
 def combine_kernel(
-    rows, first, chunk,
+    rows, first,
     me_ref, mask_ref, recv_ref, s_ref, out_ref,
     facts32, share, near_vm, near, acc, cols, near_sem,
 ):
     peers = recv_ref.shape[0]
     blocks = s_ref.shape[1] // BLOCK
     spans = -(-rows // LANES)
-    facts = recv_ref[:, CAP * rows : CAP * rows + FACTS]
-    facts32[...] = facts.astype(F32).reshape(facts32.shape)
+    facts = fact_rows(rows)
+    arrived = recv_ref[:, CAP * rows : CAP * rows + facts]
+    facts32[...] = arrived.astype(F32).reshape(facts32.shape)
 
     def fact(row):
-        return facts32[pl.ds(row, peers, stride=FACTS), :]
+        return facts32[pl.ds(row, peers, stride=facts), :]
 
     lane = iota((peers, LANES), 1)
-    routes = fact(ROUTE)
+    routes = fact(facts - 1)
     slots = jnp.zeros((peers, LANES), F32)
     for r in range(CAP):
         mine = jnp.where(lane == me_ref[0] * CAP + r, routes, 0.0)
@@ -233,7 +244,7 @@
     near_copy = pltpu.make_async_copy(near_vm, near, near_sem)
     near_copy.start()
     for q in range(spans):
-        if (q + 1) * LANES <= rows:
+        if rows - q * LANES > LANES // 2:
             values = [fact(q * VALUES + v) for v in range(VALUES)]
         else:
             values = [fact(q * VALUES + v) for v in range(VALUES // 2)]
@@ -249,27 +260,34 @@
     cols[...] = jnp.zeros(cols.shape, F32)
     near_copy.wait()
 
-    def work(q, carry):
-        at = pl.ds(pl.multiple_of(q * chunk, chunk), chunk)
+    def work(start, chunk):
+        at = pl.ds(start, chunk)
+        inner = pl.ds(0, chunk)
         shares = share[at]
-        acc[...] = jnp.zeros(acc.shape, F32)
-        for source in range(peers):
-            scale = jnp.broadcast_to(shares[:, source : source + 1], (chunk, LANES))
-            for r in range(CAP):
-                piece = recv_ref[source, pl.ds(pl.multiple_of(r * rows + q * chunk, 16), chunk)]
-                acc[near[source, r]] += scale * piece.astype(F32)
+        acc[:, inner] = jnp.zeros((blocks + 1, chunk, LANES), F32)
+
+        def sources(i, turned):
+            for j in range(GROUP):
+                source = i * GROUP + j
+                scale = jnp.broadcast_to(turned[:, j : j + 1], (chunk, LANES))
+                for r in range(CAP):
+                    piece = recv_ref[source, pl.ds(r * rows + start, chunk)]
+                    acc[near[source, r], inner] += scale * piece.astype(F32)
+            return pltpu.roll(turned, LANES - GROUP, 1)
+
+        lax.fori_loop(0, peers // GROUP, sources, shares)
         norm = jnp.broadcast_to(shares[:, peers : peers + 1], (chunk, LANES))
 
         def block(j, cross):
-            target = acc[j] + SMOOTH / VS
+            target = acc[j, inner] + SMOOTH / VS
             student = s_ref[at, pl.ds(pl.multiple_of(j * BLOCK, BLOCK), BLOCK)].astype(F32)
             return cross + target * (jnp.log(target) - (student - norm))
 
         cross = lax.fori_loop(0, blocks, block, jnp.zeros((chunk, LANES), F32))
         cols[at] = jnp.broadcast_to(jnp.sum(cross, axis=1, keepdims=True), (chunk, LANES))
-        return carry
-
-    lax.fori_loop(0, rows // chunk, work, 0)
+
+    for start in range(0, rows, acc.shape[1]):
+        work(start, min(acc.shape[1], rows - start))
     counted = jnp.sum(mask_ref[...].reshape(1, -1).astype(F32), axis=1, keepdims=True)
     row = iota((8, LANES), 0)
     place = iota((8, LANES), 1)
@@ -317,14 +335,12 @@
     loss_ref[...] = loss.reshape(loss_ref.shape)
 
 
-def close_kernel(rows, tally_ref, mean_ref, over_ref):
+def close_kernel(tally_ref, mean_ref):
     lane = iota((1, LANES), 1)
     sums = jnp.sum(tally_ref[...], axis=0, keepdims=True)
-    most = jnp.max(tally_ref[...], axis=0, keepdims=True)
     total = jnp.sum(jnp.where(lane == 0, sums, 0.0), axis=1, keepdims=True)
     count = jnp.sum(jnp.where(lane == 1, sums, 0.0), axis=1, keepdims=True)
     mean_ref[0] = jnp.sum(total / count)
-    over_ref[0] = jnp.max(jnp.where((lane == 1) & (most > rows), 1, 0))
 
 
 def whole(memory_space):
@@ -335,7 +351,7 @@
 SMALL = pltpu.CompilerParams(vmem_limit_bytes=6 << 20)
 
 
-def exchanged(teacher_logits, student_logits, dest, tile_weight, mask, rows, first):
+def exchanged(rows, first, teacher_logits, student_logits, dest, tile_weight, mask):
     peers = lax.axis_size("vocab")
     groups = lax.axis_size("dp")
     me = lax.axis_index("vocab").astype(jnp.int32).reshape(1)
@@ -343,12 +359,13 @@
     tb_dev = teacher_logits.shape[1] // BLOCK
     sb_dev = student_logits.shape[1] // BLOCK
     wide = -(-rows // LANES) * LANES
+    facts = fact_rows(rows)
     dma = pltpu.SemaphoreType.DMA
     tall = max(rows, LANES)
     send, kept = pl.pallas_call(
         functools.partial(send_kernel, rows, first, sb_dev),
         out_shape=(
-            jax.ShapeDtypeStruct((peers, CAP * rows + FACTS, LANES), BF16),
+            jax.ShapeDtypeStruct((peers, CAP * rows + facts, LANES), BF16),
             jax.ShapeDtypeStruct((rows, student_logits.shape[1]), BF16),
         ),
         in_specs=[whole(SM), whole(VM), whole(HB), whole(HB), whole(HB), whole(HB)],
@@ -375,14 +392,14 @@
         name="send",
     )(me, mask, dest, teacher_logits, tile_weight, student_logits)
     received = lax.all_to_all(send, "vocab", 0, 0, tiled=True)
-    chunk = rows // 2 if rows % 64 == 0 else rows
+    chunk = -(-rows // 32) * 16
     mine = pl.pallas_call(
-        functools.partial(combine_kernel, rows, first, chunk),
+        functools.partial(combine_kernel, rows, first),
         out_shape=jax.ShapeDtypeStruct((peers * 4, LANES), F32),
         in_specs=[whole(SM), whole(VM), whole(VM), whole(VM)],
         out_specs=whole(VM),
         scratch_shapes=[
-            VM((peers * FACTS, LANES), F32),
+            VM((peers * facts, LANES), F32),
             VM((wide, LANES), F32),
             VM((peers, LANES), jnp.int32),
             SM((peers, LANES), jnp.int32),
@@ -402,7 +419,6 @@
         compiler_params=SMALL,
         name="tally",
     )(collected)
-    tally = lax.all_to_all(tally, "dp", 0, 0, tiled=True)
     loss = pl.pallas_call(
         functools.partial(loss_kernel, rows, first),
         out_shape=jax.ShapeDtypeStruct((tokens,), F32),
@@ -412,30 +428,34 @@
         compiler_params=SMALL,
         name="loss",
     )(collected, mask)
-    mean, over = pl.pallas_call(
-        functools.partial(close_kernel, rows),
-        out_shape=(jax.ShapeDtypeStruct((1,), F32), jax.ShapeDtypeStruct((1,), jnp.int32)),
+    return loss, tally
+
+
+def local(teacher_logits, student_logits, tile_dest, tile_weight, token_mask):
+    tokens = teacher_logits.shape[0]
+    parts = (teacher_logits, student_logits, tile_dest.T, tile_weight, token_mask)
+    sizes = [tokens]
+    if tokens % 384 == 0:
+        sizes = [tokens // 384 * size for size in (304, 320, 384)]
+    which = pl.pallas_call(
+        functools.partial(size_kernel, sizes),
+        out_shape=jax.ShapeDtypeStruct((1,), jnp.int32),
         in_specs=[whole(VM)],
-        out_specs=(whole(SM), whole(SM)),
+        out_specs=whole(SM),
+        compiler_params=SMALL,
+        name="size",
+    )(token_mask)
+    loss, tally = lax.switch(which.reshape(()), [functools.partial(exchanged, size, 0) for size in sizes], *parts)
+    tally = lax.all_to_all(tally, "dp", 0, 0, tiled=True)
+    mean = pl.pallas_call(
+        close_kernel,
+        out_shape=jax.ShapeDtypeStruct((1,), F32),
+        in_specs=[whole(VM)],
+        out_specs=whole(SM),
         compiler_params=SMALL,
         name="close",
     )(tally)
-    return loss, mean.reshape(()), over.reshape(())
-
-
-def local(teacher_logits, student_logits, tile_dest, tile_weight, token_mask):
-    tokens = teacher_logits.shape[0]
-    parts = (teacher_logits, student_logits, tile_dest.T, tile_weight, token_mask)
-    rows = tokens * 5 // 6 if tokens % 384 == 0 else tokens
-    loss, mean, over = exchanged(*parts, rows, 0)
-    if rows < tokens:
-
-        def rest():
-            more, more_mean, _ = exchanged(*parts, tokens - rows, rows)
-            return loss + more, mean + more_mean
-
-        loss, mean = lax.cond(over > 0, rest, lambda: (loss, mean))
-    return loss, mean
+    return loss, mean.reshape(())
 
 
 def solution(mesh):

time: 148 us -> 144 us (0.973)
  blocking collectives: 112 us -> 122 us
  starting transfers between devices: 8.18 us -> 0 us
  waiting for transfers between devices: 6.18 us -> 0 us
    all_to_all x0 -> x1, blocking collectives: none -> 14.5 us  [local(): tally = lax.all_to_all(tally, 'dp', 0, 0, tiled=True)]
    all_to_all x1 -> x0, starting transfers between devices: 8.18 us -> none  [exchanged(): tally = lax.all_to_all(tally, 'dp', 0, 0, tiled=True)]
    all_to_all x1 -> x0, waiting for transfers between devices: 6.18 us -> none  [exchanged(): tally = lax.all_to_all(tally, 'dp', 0, 0, tiled=True)]
    all_to_all x1, blocking collectives: 99.9 us -> 96 us  [exchanged(): received = lax.all_to_all(send, 'vocab', 0, 0, tiled=True)]
    pallas_call x2 -> x3, Pallas kernels: 6.51 us -> 8.09 us  [the longest x1 6.13 us: exchanged(): pl.pallas_call(functools.partial(combine_kernel, rows, first), out_shape=...]
  transfers between devices with their start and end apart: 1 -> 0, of which waited for: 1 -> 0; matrix products, arithmetic and copies ran while one was open for 0% -> 0% of each run, Pallas kernels for 0% -> 0%
where the time goes in v5:
time: 144 us
  blocking collectives  122 us (85%)
  Pallas kernels  19.6 us (14%)
  between operations  1.49 us (1%)
    all_to_all x1, blocking collectives, exchanged(): received = lax.all_to_all(send, 'vocab', 0, 0, tiled=True)  96 us
    all_to_all x1, blocking collectives, local(): tally = lax.all_to_all(tally, 'dp', 0, 0, tiled=True)  14.5 us
    all_to_all x1, blocking collectives, exchanged(): collected = lax.all_to_all(mine, 'vocab', 0, 0, tiled=True)  11.7 us
    pallas_call x1, Pallas kernels, exchanged(): pl.pallas_call(functools.partial(send_kernel, rows, first, sb_dev), out_s...  11.2 us
    pallas_call x1, Pallas kernels, exchanged(): pl.pallas_call(functools.partial(combine_kernel, rows, first), out_shape=...  6.13 us

profile of v5, /device:TPU:1, one launch (start us, length us, event | category | flops | bytes accessed | tf_op | source)
XLA Modules:
  0.0 143.7 jit_solution(5484558277251391056)
XLA Ops:
  0.6 1.3 size.1
  2.6 125.7 %conditional.1 = (f32[384]{0:T(512)S(1)}, f32[8,128]{1,0:T(8,128)S(1)}) conditional(s32[]{:T(128)} %bitcast.9, (s32[384]{0:T(512)}, s32[2,1184]{1,0:T(2,128)}, bf16[384,4736]{1,0:T(8,128)(2,1)}, bf16[37,2,128,128]{3,2,1,0:T(8,128)(2,1)}, bf16[384,3968]{1,0:T(8,128)(2,1)}) %tuple.25, (s32[384]{0:T(512)}, s32[2,1184]{1,0:T(2,128)}, ...), branch_computations={%region_0.0_spmd, %region_1.0_spmd, %region_2.0_spmd} | conditional | flops 10000000000 | bytes 20535936 | solution.py:448
  2.6 11.2 %send.3 = (bf16[32,928,128]{2,1,0:T(8,128)(2,1)S(1)}, bf16[304,3968]{1,0:T(8,128)(2,1)S(1)}) custom-call(s32[1]{0:T(128)} %bitcast.me_ref, s32[384]{0:T(512)} %get-tuple-element.30.mask_ref, s32[2,1184]{1,0:T(2,128)} %get-tuple-element.31.dest_hbm, bf16[384,4736]{1,0:T(8,128)(2,1)} %get-tuple-element.32.x_hbm, ...), custom_call_target="tpu_custom_call" | custom-call | tf_op jit(solution)/shard_map/cond/branch_0_fun/send/pallas_call | solution.py:365
  13.8 0.0 copy-start
  13.9 96.0 %all_to_all.47.recv_ref = bf16[32,928,128]{2,1,0:T(8,128)(2,1)S(1)} all-to-all(bf16[32,928,128]{2,1,0:T(8,128)(2,1)S(1)} %get-tuple-element.35), channel_id=1, replica_groups=mesh['dp'=8,'vocab'=32] {'vocab'}, dimensions={0} | all-to-all | bytes 15204352 | tf_op jit(solution)/shard_map/cond/branch_0_fun/all_to_all | solution.py:394
  109.9 0.0 copy-done
  109.9 6.1 %combine.3 = f32[128,128]{1,0:T(8,128)S(1)} custom-call(s32[1]{0:T(128)} %bitcast.me_ref, s32[384]{0:T(512)S(1)} %copy-done, bf16[32,928,128]{2,1,0:T(8,128)(2,1)S(1)} %all_to_all.47.recv_ref, bf16[304,3968]{1,0:T(8,128)(2,1)S(1)} %get-tuple-element.36.s_ref), custom_call_target="tpu_custom_call" | custom-call | tf_op jit(solution)/shard_map/cond/branch_0_fun/combine/pallas_call | solution.py:396
  116.0 11.7 %all_to_all.48 = f32[32,4,128]{2,1,0:T(4,128)S(1)} all-to-all(f32[32,4,128]{2,1,0:T(4,128)S(1)} %bitcast.14), channel_id=1, replica_groups=mesh['dp'=8,'vocab'=32] {'vocab'}, dimensions={0} | all-to-all | bytes 131072 | tf_op jit(solution)/shard_map/cond/branch_0_fun/all_to_all | solution.py:413
  127.8 0.3 loss.3
  128.3 0.0 copy-start.3
  128.4 14.5 %all_to_all.53 = f32[8,1,128]{2,1,0:T(1,128)S(1)} all-to-all(f32[8,1,128]{2,1,0:T(1,128)S(1)} %bitcast.27), channel_id=1, replica_groups=mesh['dp'=8,'vocab'=32] {'dp'}, dimensions={0} | all-to-all | bytes 8192 | tf_op jit(solution)/shard_map/all_to_all | solution.py:449
  142.9 0.6 close.1
  143.5 0.0 copy-done.3
  (1 shorter events, 0.0 us)
Async XLA Ops:
  13.8 96.0 %copy-start = (s32[384]{0:T(512)S(1)}, s32[384]{0:T(512)}, u32[]{:S(2)}) copy-start(s32[384]{0:T(512)} %get-tuple-element.30.mask_ref) | copy-start | bytes 4612 | tf_op jit(solution)/shard_map/cond
  128.3 15.2 %copy-start.3 = (f32[384]{0:T(512)}, f32[384]{0:T(512)S(1)}, u32[]{:S(2)}) copy-start(f32[384]{0:T(512)S(1)} %get-tuple-element.53) | copy-start | bytes 4612

commit v6 on v5

--- a/solution.py
+++ b/solution.py
@@ -13,7 +13,8 @@
 CAP = 3
 SMOOTH = 0.1
 LANES = 128
-GROUP = 8
+GROUP = 12
+SOURCES = 32
 VALUES = 6
 F32 = jnp.float32
 BF16 = jnp.bfloat16
@@ -57,16 +58,23 @@
     return out
 
 
-def column_copies(hbm, buf, sems, blocks, parts):
+def column_copies(hbm, buf, sems, blocks, parts, beside=None):
     groups = blocks // GROUP
     cuts = [groups * i // parts for i in range(parts + 1)]
     out = []
     for c, (lo, hi) in enumerate(zip(cuts[:-1], cuts[1:])):
         end = hi * GROUP if c < parts - 1 else blocks
+        copies = []
+        if beside:
+            run = pl.ds(lo * GROUP, end - lo * GROUP)
+            copies.append(
+                pltpu.make_async_copy(beside[0].at[run], beside[1].at[run], beside[2].at[c])
+            )
         where = (slice(None), pl.ds(lo * GROUP * BLOCK, (end - lo * GROUP) * BLOCK))
-        copy = pltpu.make_async_copy(hbm.at[where], buf.at[where], sems.at[c])
-        copy.start()
-        out.append(((lo, hi), copy))
+        copies.append(pltpu.make_async_copy(hbm.at[where], buf.at[where], sems.at[c]))
+        for copy in copies:
+            copy.start()
+        out.append(((lo, hi), *copies))
     return out
 
 
@@ -91,16 +99,14 @@
     me_ref, mask_ref, dest_hbm, x_hbm, w_hbm, s_hbm, send_ref, kept,
     x_buf, w_buf, s_buf, dest, sel, xc, maps, cols,
     top, total, s_top, s_total, used,
-    in_sem, x_sem, s_sem,
+    in_sem, w_sem, x_sem, s_sem,
 ):
     blocks = w_buf.shape[0]
     s_blocks = s_buf.shape[1] // BLOCK
     peers = send_ref.shape[0]
-    w_copy = pltpu.make_async_copy(w_hbm, w_buf, in_sem.at[0])
-    w_copy.start()
-    x_copies = column_copies(x_hbm, x_buf, x_sem, blocks, 3)
+    x_copies = column_copies(x_hbm, x_buf, x_sem, blocks, 3, (w_hbm, w_buf, w_sem))
     ((_, s_copy),) = column_copies(s_hbm, s_buf, s_sem, s_blocks, 1)
-    dest_copy = pltpu.make_async_copy(dest_hbm, dest, in_sem.at[1])
+    dest_copy = pltpu.make_async_copy(dest_hbm, dest, in_sem)
     dest_copy.start()
     sel[...] = selector(mask_ref[...].reshape(1, -1), rows, first)
     top[...] = jnp.full(top.shape, -jnp.inf, F32)
@@ -113,7 +119,6 @@
         return carry
 
     lax.fori_loop(0, peers, clear, 0)
-    w_copy.wait()
     ones = jnp.ones((K * BLOCK, BLOCK), BF16)
 
     def weight(b):
@@ -133,8 +138,9 @@
         teacher(i, GROUP)
         return carry
 
-    for (lo, hi), copy in x_copies:
-        copy.wait()
+    for (lo, hi), *copies in x_copies:
+        for copy in copies:
+            copy.wait()
         lax.fori_loop(lo, hi, teachers, 0)
     if blocks % GROUP:
         teacher(blocks // GROUP, blocks % GROUP)
@@ -267,23 +273,29 @@
         acc[:, inner] = jnp.zeros((blocks + 1, chunk, LANES), F32)
 
         def sources(i, turned):
-            for j in range(GROUP):
-                source = i * GROUP + j
+            for j in range(SOURCES):
+                source = i * SOURCES + j
                 scale = jnp.broadcast_to(turned[:, j : j + 1], (chunk, LANES))
                 for r in range(CAP):
                     piece = recv_ref[source, pl.ds(r * rows + start, chunk)]
                     acc[near[source, r], inner] += scale * piece.astype(F32)
-            return pltpu.roll(turned, LANES - GROUP, 1)
-
-        lax.fori_loop(0, peers // GROUP, sources, shares)
+            return pltpu.roll(turned, LANES - SOURCES, 1)
+
+        lax.fori_loop(0, peers // SOURCES, sources, shares)
         norm = jnp.broadcast_to(shares[:, peers : peers + 1], (chunk, LANES))
 
         def block(j, cross):
             target = acc[j, inner] + SMOOTH / VS
-            student = s_ref[at, pl.ds(pl.multiple_of(j * BLOCK, BLOCK), BLOCK)].astype(F32)
+            start_of = j * BLOCK if isinstance(j, int) else pl.multiple_of(j * BLOCK, BLOCK)
+            student = s_ref[at, pl.ds(start_of, BLOCK)].astype(F32)
             return cross + target * (jnp.log(target) - (student - norm))
 
-        cross = lax.fori_loop(0, blocks, block, jnp.zeros((chunk, LANES), F32))
+        def two(i, cross):
+            return block(2 * i + 1, block(2 * i, cross))
+
+        cross = lax.fori_loop(0, blocks // 2, two, jnp.zeros((chunk, LANES), F32))
+        if blocks % 2:
+            cross = block(blocks - 1, cross)
         cols[at] = jnp.broadcast_to(jnp.sum(cross, axis=1, keepdims=True), (chunk, LANES))
 
     for start in range(0, rows, acc.shape[1]):
@@ -384,7 +396,8 @@
             VM((rows, LANES), F32),
             VM((rows, LANES), F32),
             SM((peers,), jnp.int32),
-            dma((2,)),
+            dma(()),
+            dma((3,)),
             dma((3,)),
             dma((1,)),
         ],

time: 144 us -> 144 us (level)
  blocking collectives: 122 us -> 125 us
  Pallas kernels: 19.6 us -> 18.1 us
    all_to_all x1, blocking collectives: 14.5 us -> 17.1 us  [local(): tally = lax.all_to_all(tally, 'dp', 0, 0, tiled=True)]
where the time goes in v6:
time: 144 us; the launch traced here: 145 us
  blocking collectives  125 us (87%)
  Pallas kernels  18.1 us (13%)
  between operations  1.49 us (1%)
    all_to_all x1, blocking collectives, exchanged(): received = lax.all_to_all(send, 'vocab', 0, 0, tiled=True)  96 us
    all_to_all x1, blocking collectives, local(): tally = lax.all_to_all(tally, 'dp', 0, 0, tiled=True)  17.1 us
    all_to_all x1, blocking collectives, exchanged(): collected = lax.all_to_all(mine, 'vocab', 0, 0, tiled=True)  11.7 us
    pallas_call x1, Pallas kernels, exchanged(): pl.pallas_call(functools.partial(send_kernel, rows, first, sb_dev), out_s...  10.6 us
    pallas_call x1, Pallas kernels, exchanged(): pl.pallas_call(functools.partial(combine_kernel, rows, first), out_shape=...  5.24 us

profile of v6, /device:TPU:1, one launch (start us, length us, event | category | flops | bytes accessed | tf_op | source)
XLA Modules:
  0.0 144.7 jit_solution(13313081625604841416)
XLA Ops:
  0.6 1.3 size.1
  2.6 124.2 %conditional.1 = (f32[384]{0:T(512)S(1)}, f32[8,128]{1,0:T(8,128)S(1)}) conditional(s32[]{:T(128)} %bitcast.9, (s32[384]{0:T(512)}, s32[2,1184]{1,0:T(2,128)}, bf16[384,4736]{1,0:T(8,128)(2,1)}, bf16[37,2,128,128]{3,2,1,0:T(8,128)(2,1)}, bf16[384,3968]{1,0:T(8,128)(2,1)}) %tuple.25, (s32[384]{0:T(512)}, s32[2,1184]{1,0:T(2,128)}, ...), branch_computations={%region_0.0_spmd, %region_1.0_spmd, %region_2.0_spmd} | conditional | flops 10000000000 | bytes 20535936 | solution.py:461
  2.6 10.6 %send.3 = (bf16[32,928,128]{2,1,0:T(8,128)(2,1)S(1)}, bf16[304,3968]{1,0:T(8,128)(2,1)S(1)}) custom-call(s32[1]{0:T(128)} %bitcast.me_ref, s32[384]{0:T(512)} %get-tuple-element.30.mask_ref, s32[2,1184]{1,0:T(2,128)} %get-tuple-element.31.dest_hbm, bf16[384,4736]{1,0:T(8,128)(2,1)} %get-tuple-element.32.x_hbm, ...), custom_call_target="tpu_custom_call" | custom-call | tf_op jit(solution)/shard_map/cond/branch_0_fun/send/pallas_call | solution.py:377
  13.2 0.0 copy-start
  13.2 96.0 %all_to_all.47.recv_ref = bf16[32,928,128]{2,1,0:T(8,128)(2,1)S(1)} all-to-all(bf16[32,928,128]{2,1,0:T(8,128)(2,1)S(1)} %get-tuple-element.35), channel_id=1, replica_groups=mesh['dp'=8,'vocab'=32] {'vocab'}, dimensions={0} | all-to-all | bytes 15204352 | tf_op jit(solution)/shard_map/cond/branch_0_fun/all_to_all | solution.py:407
  109.2 0.0 copy-done
  109.2 5.2 %combine.3 = f32[128,128]{1,0:T(8,128)S(1)} custom-call(s32[1]{0:T(128)} %bitcast.me_ref, s32[384]{0:T(512)S(1)} %copy-done, bf16[32,928,128]{2,1,0:T(8,128)(2,1)S(1)} %all_to_all.47.recv_ref, bf16[304,3968]{1,0:T(8,128)(2,1)S(1)} %get-tuple-element.36.s_ref), custom_call_target="tpu_custom_call" | custom-call | tf_op jit(solution)/shard_map/cond/branch_0_fun/combine/pallas_call | solution.py:409
  114.5 11.7 %all_to_all.48 = f32[32,4,128]{2,1,0:T(4,128)S(1)} all-to-all(f32[32,4,128]{2,1,0:T(4,128)S(1)} %bitcast.14), channel_id=1, replica_groups=mesh['dp'=8,'vocab'=32] {'vocab'}, dimensions={0} | all-to-all | bytes 131072 | tf_op jit(solution)/shard_map/cond/branch_0_fun/all_to_all | solution.py:426
  126.2 0.3 loss.3
  126.8 0.0 copy-start.3
  126.8 17.1 %all_to_all.53 = f32[8,1,128]{2,1,0:T(1,128)S(1)} all-to-all(f32[8,1,128]{2,1,0:T(1,128)S(1)} %bitcast.27), channel_id=1, replica_groups=mesh['dp'=8,'vocab'=32] {'dp'}, dimensions={0} | all-to-all | bytes 8192 | tf_op jit(solution)/shard_map/all_to_all | solution.py:462
  143.9 0.6 close.1
  144.6 0.0 copy-done.3
  (1 shorter events, 0.0 us)
Async XLA Ops:
  13.2 96.0 %copy-start = (s32[384]{0:T(512)S(1)}, s32[384]{0:T(512)}, u32[]{:S(2)}) copy-start(s32[384]{0:T(512)} %get-tuple-element.30.mask_ref) | copy-start | bytes 4612 | tf_op jit(solution)/shard_map/cond
  126.8 17.8 %copy-start.3 = (f32[384]{0:T(512)}, f32[384]{0:T(512)S(1)}, u32[]{:S(2)}) copy-start(f32[384]{0:T(512)S(1)} %get-tuple-element.53) | copy-start | bytes 4612

commit v7 on v6

--- a/solution.py
+++ b/solution.py
@@ -78,12 +78,25 @@
     return out
 
 
-def picked(sel_ref, src_ref, dst_ref, top_ref, start, count):
+def picked(band, sel_ref, src_ref, dst_ref, top_ref, start, count):
+    rows, tokens = sel_ref.shape
+    runs = [(slice(0, rows), slice(0, tokens))]
+    if band:
+        runs = [
+            (slice(r, min(r + LANES, rows)), slice(r, min(r + 2 * LANES, tokens)))
+            for r in range(0, rows, LANES)
+        ]
     tops = []
     for i in range(0, count, 2):
         width = min(2, count - i) * BLOCK
         at = pl.ds(start + i * BLOCK, width)
-        got = jnp.dot(sel_ref[...], src_ref[:, at], preferred_element_type=F32)
+        got = jnp.concatenate(
+            [
+                jnp.dot(sel_ref[r, t], src_ref[t, at], preferred_element_type=F32)
+                for r, t in runs
+            ],
+            axis=0,
+        )
         dst_ref[:, at] = got.astype(BF16)
         tops += [got[:, j : j + BLOCK] for j in range(0, width, BLOCK)]
     top_ref[...] = functools.reduce(jnp.maximum, tops, top_ref[...])
@@ -91,11 +104,14 @@
 
 def size_kernel(sizes, mask_ref, which_ref):
     kept = jnp.sum(mask_ref[...].reshape(1, -1).astype(F32))
-    which_ref[0] = sum((kept > size).astype(jnp.int32) for size in sizes[:-1]) + 0
+    which = sum((kept > size).astype(jnp.int32) for size in sizes[:-1]) + 0
+    if len(sizes) > 1:
+        which = jnp.where(kept < mask_ref.shape[0] - LANES, len(sizes) - 1, which)
+    which_ref[0] = which
 
 
 def send_kernel(
-    rows, first, sb_dev,
+    rows, first, band, sb_dev,
     me_ref, mask_ref, dest_hbm, x_hbm, w_hbm, s_hbm, send_ref, kept,
     x_buf, w_buf, s_buf, dest, sel, xc, maps, cols,
     top, total, s_top, s_total, used,
@@ -130,7 +146,7 @@
         start = i * GROUP * BLOCK
         if not isinstance(i, int):
             start = pl.multiple_of(start, GROUP * BLOCK)
-        picked(sel, x_buf, xc, top, start, count)
+        picked(band, sel, x_buf, xc, top, start, count)
         for j in range(count):
             weight(i * GROUP + j)
 
@@ -176,7 +192,7 @@
         return tile(2 * i + 1, two, tile(2 * i, one, route))
 
     def both(i, route):
-        picked(sel, s_buf, kept, s_top, pl.multiple_of(i * 4 * BLOCK, 4 * BLOCK), 4)
+        picked(band, sel, s_buf, kept, s_top, pl.multiple_of(i * 4 * BLOCK, 4 * BLOCK), 4)
         return pair(2 * i + 1, pair(2 * i, route))
 
     shared = min(blocks, s_blocks) // 4 * 2
@@ -184,7 +200,7 @@
     for i in range(shared, blocks // 2):
         route = pair(i, route)
     for b in range(2 * shared, s_blocks, 2):
-        picked(sel, s_buf, kept, s_top, b * BLOCK, min(2, s_blocks - b))
+        picked(band, sel, s_buf, kept, s_top, b * BLOCK, min(2, s_blocks - b))
     if blocks % 2:
         last = raised(blocks - 1)
         total[...] += last
@@ -363,7 +379,8 @@
 SMALL = pltpu.CompilerParams(vmem_limit_bytes=6 << 20)
 
 
-def exchanged(rows, first, teacher_logits, student_logits, dest, tile_weight, mask):
+def exchanged(rows, band, teacher_logits, student_logits, dest, tile_weight, mask):
+    first = 0
     peers = lax.axis_size("vocab")
     groups = lax.axis_size("dp")
     me = lax.axis_index("vocab").astype(jnp.int32).reshape(1)
@@ -375,7 +392,7 @@
     dma = pltpu.SemaphoreType.DMA
     tall = max(rows, LANES)
     send, kept = pl.pallas_call(
-        functools.partial(send_kernel, rows, first, sb_dev),
+        functools.partial(send_kernel, rows, first, band, sb_dev),
         out_shape=(
             jax.ShapeDtypeStruct((peers, CAP * rows + facts, LANES), BF16),
             jax.ShapeDtypeStruct((rows, student_logits.shape[1]), BF16),
@@ -458,7 +475,7 @@
         compiler_params=SMALL,
         name="size",
     )(token_mask)
-    loss, tally = lax.switch(which.reshape(()), [functools.partial(exchanged, size, 0) for size in sizes], *parts)
+    loss, tally = lax.switch(which.reshape(()), [functools.partial(exchanged, size, size < tokens) for size in sizes], *parts)
     tally = lax.all_to_all(tally, "dp", 0, 0, tiled=True)
     mean = pl.pallas_call(
         close_kernel,

time: 144 us -> 141 us (0.979)
  blocking collectives: 125 us -> 122 us
    all_to_all x1, blocking collectives: 17.1 us -> 14.5 us  [local(): tally = lax.all_to_all(tally, 'dp', 0, 0, tiled=True)]
where the time goes in v7:
time: 141 us
  blocking collectives  122 us (87%)
  Pallas kernels  17 us (12%)
  between operations  1.49 us (1%)
    all_to_all x1, blocking collectives, exchanged(): received = lax.all_to_all(send, 'vocab', 0, 0, tiled=True)  96 us
    all_to_all x1, blocking collectives, local(): tally = lax.all_to_all(tally, 'dp', 0, 0, tiled=True)  14.5 us
    all_to_all x1, blocking collectives, exchanged(): collected = lax.all_to_all(mine, 'vocab', 0, 0, tiled=True)  11.7 us
    pallas_call x1, Pallas kernels, exchanged(): pl.pallas_call(functools.partial(send_kernel, rows, first, band, sb_dev),...  9.48 us
    pallas_call x1, Pallas kernels, exchanged(): pl.pallas_call(functools.partial(combine_kernel, rows, first), out_shape=...  5.24 us

profile of v7, /device:TPU:1, one launch (start us, length us, event | category | flops | bytes accessed | tf_op | source)
XLA Modules:
  0.0 141.1 jit_solution(6613499154393026946)
XLA Ops:
  0.6 1.3 size.1
  2.6 123.1 %conditional.1 = (f32[384]{0:T(512)S(1)}, f32[8,128]{1,0:T(8,128)S(1)}) conditional(s32[]{:T(128)} %bitcast.9, (s32[384]{0:T(512)}, s32[2,1184]{1,0:T(2,128)}, bf16[384,4736]{1,0:T(8,128)(2,1)}, bf16[37,2,128,128]{3,2,1,0:T(8,128)(2,1)}, bf16[384,3968]{1,0:T(8,128)(2,1)}) %tuple.25, (s32[384]{0:T(512)}, s32[2,1184]{1,0:T(2,128)}, ...), branch_computations={%region_0.0_spmd, %region_1.0_spmd, %region_2.0_spmd} | conditional | flops 10000000000 | bytes 20535936 | solution.py:478
  2.6 9.5 %send.3 = (bf16[32,928,128]{2,1,0:T(8,128)(2,1)S(1)}, bf16[304,3968]{1,0:T(8,128)(2,1)S(1)}) custom-call(s32[1]{0:T(128)} %bitcast.me_ref, s32[384]{0:T(512)} %get-tuple-element.30.mask_ref, s32[2,1184]{1,0:T(2,128)} %get-tuple-element.31.dest_hbm, bf16[384,4736]{1,0:T(8,128)(2,1)} %get-tuple-element.32.x_hbm, ...), custom_call_target="tpu_custom_call" | custom-call | tf_op jit(solution)/shard_map/cond/branch_0_fun/send/pallas_call | solution.py:394
  12.1 0.0 copy-start
  12.1 96.0 %all_to_all.47.recv_ref = bf16[32,928,128]{2,1,0:T(8,128)(2,1)S(1)} all-to-all(bf16[32,928,128]{2,1,0:T(8,128)(2,1)S(1)} %get-tuple-element.35), channel_id=1, replica_groups=mesh['dp'=8,'vocab'=32] {'vocab'}, dimensions={0} | all-to-all | bytes 15204352 | tf_op jit(solution)/shard_map/cond/branch_0_fun/all_to_all | solution.py:424
  108.2 0.0 copy-done
  108.2 5.2 %combine.3 = f32[128,128]{1,0:T(8,128)S(1)} custom-call(s32[1]{0:T(128)} %bitcast.me_ref, s32[384]{0:T(512)S(1)} %copy-done, bf16[32,928,128]{2,1,0:T(8,128)(2,1)S(1)} %all_to_all.47.recv_ref, bf16[304,3968]{1,0:T(8,128)(2,1)S(1)} %get-tuple-element.36.s_ref), custom_call_target="tpu_custom_call" | custom-call | tf_op jit(solution)/shard_map/cond/branch_0_fun/combine/pallas_call | solution.py:426
  113.4 11.7 %all_to_all.48 = f32[32,4,128]{2,1,0:T(4,128)S(1)} all-to-all(f32[32,4,128]{2,1,0:T(4,128)S(1)} %bitcast.14), channel_id=1, replica_groups=mesh['dp'=8,'vocab'=32] {'vocab'}, dimensions={0} | all-to-all | bytes 131072 | tf_op jit(solution)/shard_map/cond/branch_0_fun/all_to_all | solution.py:443
  125.1 0.3 loss.3
  125.7 0.0 copy-start.3
  125.7 14.5 %all_to_all.53 = f32[8,1,128]{2,1,0:T(1,128)S(1)} all-to-all(f32[8,1,128]{2,1,0:T(1,128)S(1)} %bitcast.27), channel_id=1, replica_groups=mesh['dp'=8,'vocab'=32] {'dp'}, dimensions={0} | all-to-all | bytes 8192 | tf_op jit(solution)/shard_map/all_to_all | solution.py:479
  140.2 0.6 close.1
  140.9 0.0 copy-done.3
  (1 shorter events, 0.0 us)
Async XLA Ops:
  12.1 96.0 %copy-start = (s32[384]{0:T(512)S(1)}, s32[384]{0:T(512)}, u32[]{:S(2)}) copy-start(s32[384]{0:T(512)} %get-tuple-element.30.mask_ref) | copy-start | bytes 4612 | tf_op jit(solution)/shard_map/cond
  125.7 15.2 %copy-start.3 = (f32[384]{0:T(512)}, f32[384]{0:T(512)S(1)}, u32[]{:S(2)}) copy-start(f32[384]{0:T(512)S(1)} %get-tuple-element.53) | copy-start | bytes 4612

commit v8 on v7

--- a/solution.py
+++ b/solution.py
@@ -15,6 +15,7 @@
 LANES = 128
 GROUP = 12
 SOURCES = 32
+STEP = 4
 VALUES = 6
 F32 = jnp.float32
 BF16 = jnp.bfloat16
@@ -306,12 +307,14 @@
             student = s_ref[at, pl.ds(start_of, BLOCK)].astype(F32)
             return cross + target * (jnp.log(target) - (student - norm))
 
-        def two(i, cross):
-            return block(2 * i + 1, block(2 * i, cross))
-
-        cross = lax.fori_loop(0, blocks // 2, two, jnp.zeros((chunk, LANES), F32))
-        if blocks % 2:
-            cross = block(blocks - 1, cross)
+        def step(i, cross):
+            for j in range(STEP):
+                cross = block(i * STEP + j, cross)
+            return cross
+
+        cross = lax.fori_loop(0, blocks // STEP, step, jnp.zeros((chunk, LANES), F32))
+        for j in range(blocks // STEP * STEP, blocks):
+            cross = block(j, cross)
         cols[at] = jnp.broadcast_to(jnp.sum(cross, axis=1, keepdims=True), (chunk, LANES))
 
     for start in range(0, rows, acc.shape[1]):

time: 141 us -> 141 us (level)
  no operation moved by 1% of the time
where the time goes in v8:
time: 141 us
  blocking collectives  122 us (87%)
  Pallas kernels  16.9 us (12%)
  between operations  1.49 us (1%)
    all_to_all x1, blocking collectives, exchanged(): received = lax.all_to_all(send, 'vocab', 0, 0, tiled=True)  96 us
    all_to_all x1, blocking collectives, local(): tally = lax.all_to_all(tally, 'dp', 0, 0, tiled=True)  14.5 us
    all_to_all x1, blocking collectives, exchanged(): collected = lax.all_to_all(mine, 'vocab', 0, 0, tiled=True)  11.7 us
    pallas_call x1, Pallas kernels, exchanged(): pl.pallas_call(functools.partial(send_kernel, rows, first, band, sb_dev),...  9.48 us
    pallas_call x1, Pallas kernels, exchanged(): pl.pallas_call(functools.partial(combine_kernel, rows, first), out_shape=...  5.12 us

profile of v8, /device:TPU:1, one launch (start us, length us, event | category | flops | bytes accessed | tf_op | source)
XLA Modules:
  0.0 140.9 jit_solution(4315056549683823879)
XLA Ops:
  0.6 1.3 size.1
  2.6 123.0 %conditional.1 = (f32[384]{0:T(512)S(1)}, f32[8,128]{1,0:T(8,128)S(1)}) conditional(s32[]{:T(128)} %bitcast.9, (s32[384]{0:T(512)}, s32[2,1184]{1,0:T(2,128)}, bf16[384,4736]{1,0:T(8,128)(2,1)}, bf16[37,2,128,128]{3,2,1,0:T(8,128)(2,1)}, bf16[384,3968]{1,0:T(8,128)(2,1)}) %tuple.25, (s32[384]{0:T(512)}, s32[2,1184]{1,0:T(2,128)}, ...), branch_computations={%region_0.0_spmd, %region_1.0_spmd, %region_2.0_spmd} | conditional | flops 10000000000 | bytes 20535936 | solution.py:481
  2.6 9.5 %send.3 = (bf16[32,928,128]{2,1,0:T(8,128)(2,1)S(1)}, bf16[304,3968]{1,0:T(8,128)(2,1)S(1)}) custom-call(s32[1]{0:T(128)} %bitcast.me_ref, s32[384]{0:T(512)} %get-tuple-element.30.mask_ref, s32[2,1184]{1,0:T(2,128)} %get-tuple-element.31.dest_hbm, bf16[384,4736]{1,0:T(8,128)(2,1)} %get-tuple-element.32.x_hbm, ...), custom_call_target="tpu_custom_call" | custom-call | tf_op jit(solution)/shard_map/cond/branch_0_fun/send/pallas_call | solution.py:397
  12.1 0.0 copy-start
  12.1 96.0 %all_to_all.47.recv_ref = bf16[32,928,128]{2,1,0:T(8,128)(2,1)S(1)} all-to-all(bf16[32,928,128]{2,1,0:T(8,128)(2,1)S(1)} %get-tuple-element.35), channel_id=1, replica_groups=mesh['dp'=8,'vocab'=32] {'vocab'}, dimensions={0} | all-to-all | bytes 15204352 | tf_op jit(solution)/shard_map/cond/branch_0_fun/all_to_all | solution.py:427
  108.2 0.0 copy-done
  108.2 5.1 %combine.3 = f32[128,128]{1,0:T(8,128)S(1)} custom-call(s32[1]{0:T(128)} %bitcast.me_ref, s32[384]{0:T(512)S(1)} %copy-done, bf16[32,928,128]{2,1,0:T(8,128)(2,1)S(1)} %all_to_all.47.recv_ref, bf16[304,3968]{1,0:T(8,128)(2,1)S(1)} %get-tuple-element.36.s_ref), custom_call_target="tpu_custom_call" | custom-call | tf_op jit(solution)/shard_map/cond/branch_0_fun/combine/pallas_call | solution.py:429
  113.3 11.7 %all_to_all.48 = f32[32,4,128]{2,1,0:T(4,128)S(1)} all-to-all(f32[32,4,128]{2,1,0:T(4,128)S(1)} %bitcast.14), channel_id=1, replica_groups=mesh['dp'=8,'vocab'=32] {'vocab'}, dimensions={0} | all-to-all | bytes 131072 | tf_op jit(solution)/shard_map/cond/branch_0_fun/all_to_all | solution.py:446
  125.0 0.3 loss.3
  125.6 0.0 copy-start.3
  125.6 14.5 %all_to_all.53 = f32[8,1,128]{2,1,0:T(1,128)S(1)} all-to-all(f32[8,1,128]{2,1,0:T(1,128)S(1)} %bitcast.27), channel_id=1, replica_groups=mesh['dp'=8,'vocab'=32] {'dp'}, dimensions={0} | all-to-all | bytes 8192 | tf_op jit(solution)/shard_map/all_to_all | solution.py:482
  140.1 0.6 close.1
  140.8 0.0 copy-done.3
  (1 shorter events, 0.0 us)
Async XLA Ops:
  12.1 96.0 %copy-start = (s32[384]{0:T(512)S(1)}, s32[384]{0:T(512)}, u32[]{:S(2)}) copy-start(s32[384]{0:T(512)} %get-tuple-element.30.mask_ref) | copy-start | bytes 4612 | tf_op jit(solution)/shard_map/cond
  125.6 15.2 %copy-start.3 = (f32[384]{0:T(512)}, f32[384]{0:T(512)S(1)}, u32[]{:S(2)}) copy-start(f32[384]{0:T(512)S(1)} %get-tuple-element.53) | copy-start | bytes 4612
